TPU v7x, 256 devices: a whole 4x4x8 slice. The times are simulated.
256 devices in a mesh: leaf: 64 (over x, z, core), col: 4 (over y).
Axes of the slice: x: 4, y: 4, z: 8, core: 2. Of those that a mesh axis runs over, the one named last changes fastest.
Arguments:
- right_side: bfloat16 [131072, 256], P('leaf'), may hold values from -6 to 6
- x_blocks: bfloat16 [64, 4, 96, 128, 128], P('leaf', 'col'), may hold values from -0.109375 to 0.109375
- row_ids: int32 [64, 4, 96], P('leaf', 'col'), may hold values from 0 to 15
- col_ids: int32 [64, 4, 96], P('leaf', 'col'), may hold values from 0 to 13
- counts: int32 [64, 4], P('leaf', 'col'), may hold values from 48 to 96, as said below
Outputs:
- solution: bfloat16 [131072, 256], P(('leaf', 'col'))
Inputs may be any that keep to these rules, and one draw needn't show every extreme that they name: `row_ids`: block rows index the rows of the device's own subtree. `col_ids`: slots below 2 are the subtree's own columns; slot 2 + (l - 1) * 2 + s is column s of the level-l separator. `counts`: some device uses all 96 slots; slots past a device's count are unused.
All inputs are finite; a program needn't handle non-finite values.
Results may differ from a plain program's by a relative error of at most 0.0047.
Values may be sent and summed in bfloat16 or wider, within the bound.
A program may use at most 128 MiB of HBM per device.

v0:
```python
import jax
import jax.numpy as jnp
from jax import lax
from jax.sharding import PartitionSpec as P

CI = 2
SEP = 2


def from_partner(x, axis, apart):
    return lax.ppermute(x, axis, [(i, i ^ 1 << apart) for i in range(lax.axis_size(axis))])


def body(right_side, x_blocks, row_ids, col_ids, counts):
    blocks = x_blocks[0, 0]
    block_rows = row_ids[0, 0]
    block_cols = col_ids[0, 0]
    live_count = counts[0, 0]
    list_len = blocks.shape[0]
    block_size = blocks.shape[1]
    columns = right_side.shape[1]
    row_blocks = right_side.shape[0] // block_size
    levels = lax.axis_size("leaf").bit_length() - 1
    slot_total = CI + levels * SEP
    alive_weight = (lax.iota(jnp.int32, list_len) < live_count).astype(jnp.float32)[:, None, None]
    rhs_blocks = right_side.reshape(row_blocks, block_size, columns)
    picked = rhs_blocks[block_rows]
    products = jnp.einsum("kab,kac->kbc", blocks, picked, preferred_element_type=jnp.float32)
    partial_value = (
        jnp.zeros((slot_total, block_size, columns), jnp.float32)
        .at[block_cols]
        .add(products * alive_weight)
    )
    interior = partial_value[:CI]
    separators = partial_value[CI:].reshape(levels, SEP, block_size, columns)
    for level_bit in range(levels):
        pending = separators[level_bit:]
        incoming = from_partner(pending, "leaf", level_bit)
        separators = jnp.concatenate([separators[:level_bit], pending + incoming], axis=0)
    finished_seps = separators.reshape(levels * SEP, block_size, columns)
    coarse = jnp.concatenate([interior, finished_seps], axis=0).astype(jnp.bfloat16)
    gathered = coarse[block_cols]
    image = jnp.einsum("kab,kbc->kac", blocks, gathered, preferred_element_type=jnp.float32)
    terms = (
        jnp.zeros((row_blocks, block_size, columns), jnp.float32)
        .at[block_rows]
        .add(image * alive_weight)
    )
    terms = terms.reshape(row_blocks * block_size, columns)
    return lax.psum_scatter(terms, "col", scatter_dimension=0, tiled=True).astype(jnp.bfloat16)


def solution(mesh):
    in_specs = (
        P("leaf", None),
        P("leaf", "col", None, None, None),
        P("leaf", "col", None),
        P("leaf", "col", None),
        P("leaf", "col"),
    )
    out_specs = P(("leaf", "col"), None)
    return jax.shard_map(body, mesh=mesh, in_specs=in_specs, out_specs=out_specs, check_vma=False)
```

profile of v0, /device:TPU:1, one launch (start us, length us, event | category | flops | bytes accessed | tf_op | source)
XLA Modules:
  0.0 317.6 jit_solution(11215254030563688723)
XLA Ops:
  6.5 0.0 copy-start
  6.5 0.0 reduce-scatter.2.cloned.1.call-start
  6.5 0.8 fusion.8
  8.2 7.2 %gather_fusion = bf16[96,128,256]{2,1,0:T(8,128)(2,1)} fusion(bf16[16,128,256]{2,1,0:T(8,128)(2,1)} %bitcast.26, s32[1024]{0:T(1024)S(1)} %pad_clamp_fusion.1), kind=kCustom, calls=%fused_computation | custom fusion | bytes 12583296 | tf_op jit(solution)/shard_map/gather | solution.py:27
  15.4 0.0 copy-done
  15.4 9.8 %multiply_bitcast_fusion.1 = f32[96,128,256]{1,2,0:T(8,128)} fusion(f32[96]{0:T(128)S(1)} %compare_convert_fusion, bf16[96,128,256]{2,1,0:T(8,128)(2,1)} %gather_fusion, bf16[1,1,96,128,128]{4,3,2,1,0:T(8,128)(2,1)S(1)} %copy-done), kind=kOutput, calls=%fused_computation.5 | convolution fusion | flops 808452096 | bytes 22020480 | tf_op jit(solution)/shard_map/kab,kac->kbc/dot_general | solution.py:28
  25.2 0.0 copy-start.1
  25.2 12.6 %copy.9 = f32[96,128,256]{2,1,0:T(8,128)} copy(f32[96,128,256]{1,2,0:T(8,128)} %multiply_bitcast_fusion.1) | data formatting | bytes 25165824 | tf_op jit(solution)/shard_map/mul | solution.py:32
  37.8 0.0 copy-done.1
  37.8 1.5 broadcast_in_dim.5
  39.3 28.0 %scatter_fusion = f32[14,128,256]{2,1,0:T(8,128)} fusion(f32[14,128,256]{2,1,0:T(8,128)} %broadcast_in_dim.5, s32[96]{0:T(128)S(1)} %fusion.9, f32[96,128,256]{2,1,0:T(8,128)} %copy.9), kind=kCustom, calls=%fused_computation.2 | custom fusion | flops 3145728 | bytes 37749120 | tf_op jit(solution)/shard_map/scatter-add | solution.py:32
  67.3 1.5 slice.59
  68.8 3.5 %collective-permute-start = (f32[6,2,128,256]{3,2,1,0:T(8,128)S(1)}, f32[6,2,128,256]{3,2,1,0:T(8,128)S(1)}, u32[]{:S(2)}, u32[]{:S(2)}) collective-permute-start(f32[6,2,128,256]{3,2,1,0:T(8,128)S(1)} %bitcast.27), channel_id=1, source_target_pairs={{0,4},{4,0},{8,12},{12,8},{16,20},{20,16},{24,28},{28,24},{32,36},... | collective-permute-start | bytes 4718600 | tf_op jit(solution)/shard_map/ppermute | solution.py:11
  72.3 3.0 collective-permute-done
  75.4 0.2 add.48
  75.6 0.1 slice.61
  75.7 0.1 collective-permute-start.1
  75.8 29.9 %collective-permute-done.1 = f32[5,2,128,256]{3,2,1,0:T(8,128)S(1)} collective-permute-done((f32[5,2,128,256]{3,2,1,0:T(8,128)S(1)}, f32[5,2,128,256]{3,2,1,0:T(8,128)S(1)}, u32[]{:S(2)}, u32[]{:S(2)}) %collective-permute-start.1) | collective-permute-done | bytes 1310752 | tf_op jit(solution)/shard_map/ppermute | solution.py:11
  105.7 0.2 fusion.11
  105.9 0.1 slice.62
  106.0 1.1 collective-permute-start.2
  107.2 47.3 %collective-permute-done.2 = f32[4,2,128,256]{3,2,1,0:T(8,128)S(1)} collective-permute-done((f32[4,2,128,256]{3,2,1,0:T(8,128)S(1)}, f32[4,2,128,256]{3,2,1,0:T(8,128)S(1)}, u32[]{:S(2)}, u32[]{:S(2)}) %collective-permute-start.2) | collective-permute-done | bytes 1048608 | tf_op jit(solution)/shard_map/ppermute | solution.py:11
  154.5 0.2 fusion.12
  154.7 0.1 slice.63
  154.7 5.1 %collective-permute-start.3 = (f32[3,2,128,256]{3,2,1,0:T(8,128)S(1)}, f32[3,2,128,256]{3,2,1,0:T(8,128)S(1)}, u32[]{:S(2)}, u32[]{:S(2)}) collective-permute-start(f32[3,2,128,256]{3,2,1,0:T(8,128)S(1)} %slice.63), channel_id=1, source_target_pairs={{0,32},{4,36},{8,40},{12,44},{16,48},{20,52},{24,56},{28,60},{32,0... | collective-permute-start | bytes 2359304 | tf_op jit(solution)/shard_map/ppermute | solution.py:11
  159.8 34.6 %collective-permute-done.3 = f32[3,2,128,256]{3,2,1,0:T(8,128)S(1)} collective-permute-done((f32[3,2,128,256]{3,2,1,0:T(8,128)S(1)}, f32[3,2,128,256]{3,2,1,0:T(8,128)S(1)}, u32[]{:S(2)}, u32[]{:S(2)}) %collective-permute-start.3) | collective-permute-done | bytes 786464 | tf_op jit(solution)/shard_map/ppermute | solution.py:11
  194.4 0.1 fusion.10
  194.6 0.1 collective-permute-start.4
  194.7 12.1 %collective-permute-done.4 = f32[2,2,128,256]{3,2,1,0:T(8,128)S(1)} collective-permute-done((f32[2,2,128,256]{3,2,1,0:T(8,128)S(1)}, f32[2,2,128,256]{3,2,1,0:T(8,128)S(1)}, u32[]{:S(2)}, u32[]{:S(2)}) %collective-permute-start.4) | collective-permute-done | bytes 524320 | tf_op jit(solution)/shard_map/ppermute | solution.py:11
  206.7 0.1 fusion.13
  206.8 1.1 collective-permute-start.5
  208.0 1.0 slice.74
  209.0 0.1 fusion.5
  209.1 5.1 %collective-permute-done.5 = f32[1,2,128,256]{3,2,1,0:T(8,128)S(1)} collective-permute-done((f32[1,2,128,256]{3,2,1,0:T(8,128)S(1)}, f32[1,2,128,256]{3,2,1,0:T(8,128)S(1)}, u32[]{:S(2)}, u32[]{:S(2)}) %collective-permute-start.5) | collective-permute-done | bytes 262176 | tf_op jit(solution)/shard_map/ppermute | solution.py:11
  214.3 0.1 pad_maximum_fusion.1
  214.3 1.0 pad_maximum_fusion
  215.4 7.2 %gather_fusion.1 = bf16[96,128,256]{2,1,0:T(8,128)(2,1)} fusion(bf16[14,128,256]{2,1,0:T(8,128)(2,1)} %pad_maximum_fusion, s32[1024]{0:T(1024)S(1)} %pad_clamp_fusion), kind=kCustom, calls=%fused_computation.1 | custom fusion | bytes 12583296 | tf_op jit(solution)/shard_map/gather | solution.py:42
  222.6 9.9 %multiply_bitcast_fusion = f32[96,128,256]{1,2,0:T(8,128)} fusion(f32[96]{0:T(128)S(1)} %compare_convert_fusion, bf16[96,128,256]{2,1,0:T(8,128)(2,1)} %gather_fusion.1, bf16[1,1,96,128,128]{4,3,2,1,0:T(8,128)(2,1)S(1)} %copy-done), kind=kOutput, calls=%fused_computation.4 | convolution fusion | flops 808452096 | bytes 22020480 | tf_op jit(solution)/shard_map/kab,kbc->kac/dot_general | solution.py:43
  232.4 12.6 %copy.11 = f32[96,128,256]{2,1,0:T(8,128)} copy(f32[96,128,256]{1,2,0:T(8,128)} %multiply_bitcast_fusion) | data formatting | bytes 25165824 | tf_op jit(solution)/shard_map/mul | solution.py:47
  245.0 1.6 broadcast_in_dim.4
  246.6 28.2 %scatter_fusion.1 = f32[16,128,256]{2,1,0:T(8,128)} fusion(f32[16,128,256]{2,1,0:T(8,128)} %broadcast_in_dim.4, s32[96]{0:T(128)S(1)} %fusion.8, f32[96,128,256]{2,1,0:T(8,128)} %copy.11), kind=kCustom, calls=%fused_computation.3 | custom fusion | flops 3145728 | bytes 37749120 | tf_op jit(solution)/shard_map/scatter-add | solution.py:47
  274.7 0.0 reduce-scatter.2.cloned.1.call-update
  274.8 34.2 %reduce-scatter.2.cloned.1.call-done = f32[512,256]{1,0:T(8,128)} async-done(((f32[2048,256]{1,0:T(8,128)}), f32[512,256]{1,0:T(8,128)}) %reduce-scatter.2.cloned.1.call-update) | async-done | bytes 524304 | tf_op jit(solution)/shard_map/reduce_scatter | solution.py:50
  309.0 1.8 convert_element_type.12
  (9 shorter events, 0.2 us)
Async XLA Ops:
  6.5 8.8 %copy-start = (bf16[1,1,96,128,128]{4,3,2,1,0:T(8,128)(2,1)S(1)}, bf16[1,1,96,128,128]{4,3,2,1,0:T(8,128)(2,1)}, u32[]{:S(2)}) copy-start(bf16[1,1,96,128,128]{4,3,2,1,0:T(8,128)(2,1)} %param.6) | copy-start | bytes 9437188
  6.5 302.4 %reduce-scatter.2.cloned.1.call-start = ((), (), s32[]{:S(2)}) async-start(), calls=%async_computation.1 | async-start | bytes 2621440 | tf_op jit(solution)/shard_map/reduce_scatter | solution.py:50
  25.2 12.6 %copy-start.1 = (s32[1,1,96]{2,1,0:T(1,128)S(1)}, s32[1,1,96]{2,1,0:T(1,128)}, u32[]{:S(2)}) copy-start(s32[1,1,96]{2,1,0:T(1,128)} %param.8) | copy-start | bytes 1156
  68.8 6.6 %collective-permute-start = (f32[6,2,128,256]{3,2,1,0:T(8,128)S(1)}, f32[6,2,128,256]{3,2,1,0:T(8,128)S(1)}, u32[]{:S(2)}, u32[]{:S(2)}) collective-permute-start(f32[6,2,128,256]{3,2,1,0:T(8,128)S(1)} %bitcast.27), channel_id=1, source_target_pairs={{0,4},{4,0},{8,12},{12,8},{16,20},{20,16},{24,28},{28,24},{32,36},... | collective-permute-start | bytes 4718600 | tf_op jit(solution)/shard_map/ppermute | solution.py:11
  75.7 30.1 %collective-permute-start.1 = (f32[5,2,128,256]{3,2,1,0:T(8,128)S(1)}, f32[5,2,128,256]{3,2,1,0:T(8,128)S(1)}, u32[]{:S(2)}, u32[]{:S(2)}) collective-permute-start(f32[5,2,128,256]{3,2,1,0:T(8,128)S(1)} %slice.61), channel_id=1, source_target_pairs={{0,8},{4,12},{8,0},{12,4},{16,24},{20,28},{24,16},{28,20},{32,40},... | collective-permute-start | bytes 3932168 | tf_op jit(solution)/shard_map/ppermute | solution.py:11
  106.0 48.5 %collective-permute-start.2 = (f32[4,2,128,256]{3,2,1,0:T(8,128)S(1)}, f32[4,2,128,256]{3,2,1,0:T(8,128)S(1)}, u32[]{:S(2)}, u32[]{:S(2)}) collective-permute-start(f32[4,2,128,256]{3,2,1,0:T(8,128)S(1)} %slice.62), channel_id=1, source_target_pairs={{0,16},{4,20},{8,24},{12,28},{16,0},{20,4},{24,8},{28,12},{32,48},... | collective-permute-start | bytes 3145736 | tf_op jit(solution)/shard_map/ppermute | solution.py:11
  154.7 39.7 %collective-permute-start.3 = (f32[3,2,128,256]{3,2,1,0:T(8,128)S(1)}, f32[3,2,128,256]{3,2,1,0:T(8,128)S(1)}, u32[]{:S(2)}, u32[]{:S(2)}) collective-permute-start(f32[3,2,128,256]{3,2,1,0:T(8,128)S(1)} %slice.63), channel_id=1, source_target_pairs={{0,32},{4,36},{8,40},{12,44},{16,48},{20,52},{24,56},{28,60},{32,0... | collective-permute-start | bytes 2359304 | tf_op jit(solution)/shard_map/ppermute | solution.py:11
  194.6 12.2 %collective-permute-start.4 = (f32[2,2,128,256]{3,2,1,0:T(8,128)S(1)}, f32[2,2,128,256]{3,2,1,0:T(8,128)S(1)}, u32[]{:S(2)}, u32[]{:S(2)}) collective-permute-start(f32[2,2,128,256]{3,2,1,0:T(8,128)S(1)} %slice.64), channel_id=1, source_target_pairs={{0,64},{4,68},{8,72},{12,76},{16,80},{20,84},{24,88},{28,92},{32,9... | collective-permute-start | bytes 1572872 | tf_op jit(solution)/shard_map/ppermute | solution.py:11
  206.8 7.4 %collective-permute-start.5 = (f32[1,2,128,256]{3,2,1,0:T(8,128)S(1)}, f32[1,2,128,256]{3,2,1,0:T(8,128)S(1)}, u32[]{:S(2)}, u32[]{:S(2)}) collective-permute-start(f32[1,2,128,256]{3,2,1,0:T(8,128)S(1)} %slice.65), channel_id=1, source_target_pairs={{0,128},{4,132},{8,136},{12,140},{16,144},{20,148},{24,152},{28,15... | collective-permute-start | bytes 786440 | tf_op jit(solution)/shard_map/ppermute | solution.py:11
Sparse Core Ops, SparseCore 0:
  274.9 34.0 reduce-scatter.1
where the time goes:
time: 318 us
  waiting for transfers between devices  166 us (52%)
  other arithmetic  60.8 us (19%)
  local copies, waits for them, and re-layouts  45.3 us (14%)
  matrix products  19.7 us (6%)
  between operations  14.3 us (4%)
  starting transfers between devices  11.1 us (3%)
    ppermute x6, waiting for transfers between devices, from_partner(): lax.ppermute(x, axis, [(i, i ^ 1 << apart) for i in range(lax.axis_size(a...  132 us
    reduce_scatter x1, waiting for transfers between devices, body(): lax.psum_scatter(terms, 'col', scatter_dimension=0, tiled=True)  34.2 us
    scatter-add x1, other arithmetic, body(): terms = jnp.zeros((row_blocks, block_size, columns), jnp.float32).at[bloc...  28.2 us
    scatter-add x1, other arithmetic, body(): partial_value = jnp.zeros((slot_total, block_size, columns), jnp.float32)...  28 us
    mul x1, local copies, waits for them, and re-layouts, body(): products * alive_weight  12.6 us
    mul x1, local copies, waits for them, and re-layouts, body(): image * alive_weight  12.6 us
    ppermute x6, starting transfers between devices, from_partner(): lax.ppermute(x, axis, [(i, i ^ 1 << apart) for i in range(lax.axis_size(a...  11.1 us
    dot_general x1, matrix products, body(): jnp.einsum('kab,kbc->kac', blocks, gathered, preferred_element_type=jnp.f...  9.85 us
  transfers between devices with their start and end apart: 7, of which 7 were waited for; matrix products, arithmetic and copies ran while one was open for 0% of the time, Pallas kernels for 0%

commit v1 on v0

v1 whole, which is shorter than its diff:
```python
import jax
import jax.numpy as jnp
from jax import lax
from jax.experimental import pallas as pl
from jax.experimental.pallas import tpu as pltpu
from jax.sharding import PartitionSpec as P

BLOCK = 128
ROW_BLOCKS = 16
LIST_LEN = 96
COLUMNS = 256
SLOTS = 14
ROWS = ROW_BLOCKS * BLOCK
WIDTH = SLOTS * BLOCK
Z = 8
X = 4
HALF = COLUMNS // 2
MESH = pl.DeviceIdType.MESH
GROUPS = 8
PER_GROUP = LIST_LEN // GROUPS
F32 = jnp.float32
BF16 = jnp.bfloat16


def build_kernel(row_ref, col_ref, count_ref, right_hbm, blocks_hbm, dense, right_t, right_buf, block_buf, extra, seen, sems):
    fetch_right = pltpu.make_async_copy(right_hbm, right_buf, sems.at[GROUPS])
    fetch_right.start()
    fetches = []
    for g in range(GROUPS):
        part = pl.ds(g * PER_GROUP, PER_GROUP)
        fetches.append(pltpu.make_async_copy(blocks_hbm.at[0, 0, part], block_buf.at[part], sems.at[g]))
        fetches[-1].start()

    @pl.loop(0, ROW_BLOCKS * SLOTS)
    def _(p):
        seen[p] = -1

    @pl.loop(0, ROWS // 64)
    def _(i):
        dense[pl.ds(pl.multiple_of(i * 64, 64), 64), :] = jnp.zeros((64, WIDTH), BF16)

    fetch_right.wait()

    @pl.loop(0, ROW_BLOCKS)
    def _(i):
        at = pl.multiple_of(i * BLOCK, BLOCK)
        right_t[:, pl.ds(at, BLOCK)] = right_buf[pl.ds(at, BLOCK), :].T

    count = count_ref[0, 0]
    used = jnp.int32(0)
    for g in range(GROUPS):
        fetches[g].wait()

        def add_block(k, used):
            r = row_ref[0, 0, k]
            c = col_ref[0, 0, k]
            place = r * SLOTS + c
            state = seen[place]
            rows = pl.ds(pl.multiple_of(r * BLOCK, BLOCK), BLOCK)
            cols = pl.ds(pl.multiple_of(c * BLOCK, BLOCK), BLOCK)

            @pl.when(state == -1)
            def _():
                dense[rows, cols] = block_buf[k]
                seen[place] = -2

            @pl.when(state == -2)
            def _():
                total = dense[rows, cols].astype(F32) + block_buf[k].astype(F32)
                extra[used] = total
                dense[rows, cols] = total.astype(BF16)
                seen[place] = used

            @pl.when(state >= 0)
            def _():
                total = extra[state] + block_buf[k].astype(F32)
                extra[state] = total
                dense[rows, cols] = total.astype(BF16)

            return used + jnp.where(state == -2, 1, 0)

        used = lax.fori_loop(g * PER_GROUP, jnp.clip(count, g * PER_GROUP, (g + 1) * PER_GROUP), add_block, used)


def level_lanes(level, levels=1):
    start = (2 + (level - 1) * 2) * BLOCK
    return slice(start, start + levels * 2 * BLOCK)


TOP = level_lanes(5, 2)
LOW = TOP.start


def dot_t(a, b):
    return lax.dot_general(a, b, (((1,), (1,)), ((), ())), preferred_element_type=F32)


def solve_kernel(
    dense, right_t, out,
    coarse, pair_out, pair_in, own, z_out, z_in, quad_in, next_in, x_out, x_in,
    terms, y_far, y_far_in, y_out, y_in, send, recv,
):
    leaf = lax.axis_index("leaf")
    col = lax.axis_index("col")
    core = lax.rem(leaf, 2)
    z = lax.rem(leaf // 2, Z)
    x = leaf // (2 * Z)
    quad = z // 4
    in_quad = lax.rem(z, 4)

    def at(x_to, z_to, core_to):
        return ((x_to * Z + z_to) * 2 + core_to, col)

    partner = at(x, z, 1 - core)
    z_peer = [at(x, lax.rem(z + d, Z), core) for d in range(Z)]
    quad_peer = [at(x, quad * 4 + lax.rem(in_quad + d, 4), core) for d in range(4)]
    z_next = z + 1 - 2 * lax.rem(z, 2)
    x_peer = []
    for b in range(X):
        flip_0 = x + 1 - 2 * lax.rem(x, 2) if b & 1 else x
        high = flip_0 // 2
        flip_1 = flip_0 + 2 - 4 * high if b & 2 else flip_0
        x_peer.append(at(flip_1, z, core))
    up = (leaf, lax.rem(col + 1, 4))
    down = (leaf, lax.rem(col + 3, 4))

    barrier = pltpu.get_barrier_semaphore()
    peers = [partner] + z_peer[1:] + x_peer[1:] + [up, down]
    for peer in peers:
        pl.semaphore_signal(barrier, inc=1, device_id=peer, device_id_type=MESH)

    started = []

    def copy(src, dst, to):
        n = len(started)
        c = pltpu.make_async_remote_copy(
            src_ref=src, dst_ref=dst, send_sem=send.at[n], recv_sem=recv.at[n], device_id=to, device_id_type=MESH
        )
        c.start()
        started.append(c)
        return c

    mine = pl.ds(pl.multiple_of(core * HALF, HALF), HALF)
    other = pl.ds(pl.multiple_of((1 - core) * HALF, HALF), HALF)

    def pair_start(lanes):
        value = lax.dot_general(right_t[...], dense[:, lanes], (((1,), (0,)), ((), ())), preferred_element_type=F32)
        own[:, lanes] = value
        pair_out[:, lanes] = value.astype(BF16)

    def pair_send(lanes):
        return copy(pair_out.at[other, lanes], pair_in.at[:, lanes], partner)

    def pair_sum(lanes):
        return own[mine, lanes] + pair_in[:, lanes].astype(F32)

    pair_start(TOP)
    pl.semaphore_wait(barrier, len(peers))
    pair_top = pair_send(TOP)
    low_pairs = {}
    for level in (4, 3, 2):
        pair_start(level_lanes(level))
        low_pairs[level] = pair_send(level_lanes(level))

    def keep(lanes, total):
        own[mine, lanes] = total
        z_out[:, lanes] = total.astype(BF16)

    def ring_send(lanes):
        copies = []
        for d in range(1, Z):
            rows = pl.ds(pl.multiple_of(lax.rem(z + d, Z) * 16, 16), 16)
            copies.append(copy(z_out.at[rows, lanes], z_in.at[d, :, lanes], z_peer[d]))
        return copies

    chunk = pl.ds(pl.multiple_of(core * HALF + z * 16, 16), 16)

    def ring_sum(copies, lanes):
        total = own[chunk, lanes]
        for d in range(1, Z):
            copies[d - 1].wait_recv()
            total += z_in[d, :, lanes].astype(F32)
        return total

    def ring_share(lanes):
        return [copy(coarse.at[chunk, lanes], coarse.at[chunk, lanes], z_peer[d]) for d in range(1, Z)]

    pair_top.wait_recv()
    keep(TOP, pair_sum(TOP))
    top_ring = ring_send(TOP)

    four = level_lanes(4)
    low_pairs[4].wait_recv()
    keep(four, pair_sum(four))
    four_ring = ring_send(four)

    three = level_lanes(3)
    low_pairs[3].wait_recv()
    keep(three, pair_sum(three))
    three_quad = []
    for d in range(1, 4):
        rows = pl.ds(pl.multiple_of(lax.rem(in_quad + d, 4) * 32, 32), 32)
        three_quad.append(copy(z_out.at[rows, three], quad_in.at[d], quad_peer[d]))

    two = level_lanes(2)
    low_pairs[2].wait_recv()
    keep(two, pair_sum(two))
    two_next = copy(z_out.at[:, two], next_in, at(x, z_next, core))

    one = level_lanes(1)
    pair_start(slice(0, one.stop))
    one_pair = copy(pair_out.at[:, one], y_far_in.at[2], partner)
    coarse[:, 0:one.start] = pair_out[:, 0:one.start]

    top_chunk = ring_sum(top_ring, TOP)
    x_out[...] = top_chunk
    six = slice(2 * BLOCK, 4 * BLOCK)
    x_copies = [
        copy(x_out, x_in.at[1], x_peer[1]),
        copy(x_out.at[:, six], x_in.at[2, :, six], x_peer[2]),
        copy(x_out.at[:, six], x_in.at[3, :, six], x_peer[3]),
    ]

    coarse[chunk, four] = ring_sum(four_ring, four).astype(BF16)
    four_share = ring_share(four)

    quad_rows = pl.ds(pl.multiple_of(core * HALF + in_quad * 32, 32), 32)
    total = own[quad_rows, three]
    for d in range(1, 4):
        three_quad[d - 1].wait_recv()
        total += quad_in[d].astype(F32)
    coarse[quad_rows, three] = total.astype(BF16)
    three_share = [copy(coarse.at[quad_rows, three], coarse.at[quad_rows, three], quad_peer[d]) for d in range(1, 4)]

    for c in x_copies:
        c.wait_recv()
    coarse[chunk, TOP.start:TOP.start + 2 * BLOCK] = (x_out[:, 0:2 * BLOCK] + x_in[1, :, 0:2 * BLOCK]).astype(BF16)
    coarse[chunk, TOP.start + 2 * BLOCK:TOP.stop] = (
        (x_out[:, six] + x_in[1, :, six]) + (x_in[2, :, six] + x_in[3, :, six])
    ).astype(BF16)
    top_share = ring_share(TOP)

    two_next.wait_recv()
    coarse[mine, two] = (own[mine, two] + next_in[...].astype(F32)).astype(BF16)
    give_two = copy(coarse.at[mine, two], coarse.at[mine, two], partner)
    one_pair.wait_recv()
    coarse[:, one] = (own[:, one] + y_far_in[2].astype(F32)).astype(BF16)
    for c in three_share:
        c.wait_recv()
    give_three = copy(coarse.at[mine, three], coarse.at[mine, three], partner)
    for c in four_share:
        c.wait_recv()
    give_four = copy(coarse.at[mine, four], coarse.at[mine, four], partner)
    for c in (give_two, give_three, give_four):
        c.wait_recv()

    @pl.loop(0, ROWS // 256)
    def _(i):
        rows = pl.ds(pl.multiple_of(i * 256, 256), 256)
        terms[rows, :] = dot_t(dense[rows, 0:LOW], coarse[:, 0:LOW])

    for c in top_share:
        c.wait_recv()
    give_top = copy(coarse.at[mine, TOP], coarse.at[mine, TOP], partner)
    give_top.wait_recv()

    def finish(quarter, half):
        rows = pl.ds(pl.multiple_of(quarter * 512 + half * 256, 256), 256)
        return terms[rows, :] + dot_t(dense[rows, TOP], coarse[:, TOP])

    far = lax.rem(col + 2, 4)
    above = lax.rem(col + 1, 4)
    below = lax.rem(col + 3, 4)
    y_far[0] = finish(far, 0).astype(BF16)
    far_up = copy(y_far.at[0], y_far_in.at[0], up)
    y_far[1] = finish(far, 1).astype(BF16)
    far_down = copy(y_far.at[1], y_far_in.at[1], down)
    y_out[0, 1] = finish(above, 1).astype(BF16)
    up_b = copy(y_out.at[0, 1], y_in.at[0, 1], up)
    y_out[1, 0] = finish(below, 0).astype(BF16)
    down_a = copy(y_out.at[1, 0], y_in.at[1, 0], down)
    up_value = finish(above, 0)
    far_up.wait_recv()
    y_out[0, 0] = (up_value + y_far_in[0].astype(F32)).astype(BF16)
    up_a = copy(y_out.at[0, 0], y_in.at[0, 0], up)
    down_value = finish(below, 1)
    far_down.wait_recv()
    y_out[1, 1] = (down_value + y_far_in[1].astype(F32)).astype(BF16)
    down_b = copy(y_out.at[1, 1], y_in.at[1, 1], down)
    for half in range(2):
        rows = pl.ds(pl.multiple_of(col * 512 + half * 256, 256), 256)
        terms[rows, :] = finish(col, half)
    for half, pair in ((1, (up_b, down_b)), (0, (up_a, down_a))):
        for c in pair:
            c.wait_recv()
        rows = pl.ds(pl.multiple_of(col * 512 + half * 256, 256), 256)
        total = terms[rows, :] + (y_in[0, half].astype(F32) + y_in[1, half].astype(F32))
        out[half * 256:(half + 1) * 256, :] = total.astype(BF16)
    for c in started:
        c.wait_send()


COPIES = 80


def body(right_side, x_blocks, row_ids, col_ids, counts):
    vmem = pl.BlockSpec(memory_space=pltpu.VMEM)
    smem = pl.BlockSpec(memory_space=pltpu.SMEM)
    hbm = pl.BlockSpec(memory_space=pl.ANY)
    dense, right_t = pl.pallas_call(
        build_kernel,
        out_shape=(jax.ShapeDtypeStruct((ROWS, WIDTH), BF16), jax.ShapeDtypeStruct((COLUMNS, ROWS), BF16)),
        in_specs=[smem, smem, smem, hbm, hbm],
        out_specs=(vmem, vmem),
        scratch_shapes=[
            pltpu.VMEM((ROWS, COLUMNS), BF16),
            pltpu.VMEM((LIST_LEN, BLOCK, BLOCK), BF16),
            pltpu.VMEM((LIST_LEN // 2, BLOCK, BLOCK), F32),
            pltpu.SMEM((ROW_BLOCKS * SLOTS,), jnp.int32),
            pltpu.SemaphoreType.DMA((GROUPS + 1,)),
        ],
        compiler_params=pltpu.CompilerParams(vmem_limit_bytes=20 * 2**20),
        name="build_dense",
    )(row_ids, col_ids, counts, right_side, x_blocks)
    return pl.pallas_call(
        solve_kernel,
        out_shape=jax.ShapeDtypeStruct((ROWS // 4, COLUMNS), BF16),
        in_specs=[vmem, vmem],
        out_specs=vmem,
        scratch_shapes=[
            pltpu.VMEM((COLUMNS, WIDTH), BF16),
            pltpu.VMEM((COLUMNS, WIDTH), BF16),
            pltpu.VMEM((HALF, WIDTH), BF16),
            pltpu.VMEM((COLUMNS, WIDTH), F32),
            pltpu.VMEM((HALF, WIDTH), BF16),
            pltpu.VMEM((Z, 16, WIDTH), BF16),
            pltpu.VMEM((4, 32, 2 * BLOCK), BF16),
            pltpu.VMEM((HALF, 2 * BLOCK), BF16),
            pltpu.VMEM((16, 4 * BLOCK), F32),
            pltpu.VMEM((X, 16, 4 * BLOCK), F32),
            pltpu.VMEM((ROWS, COLUMNS), F32),
            pltpu.VMEM((2, 256, COLUMNS), BF16),
            pltpu.VMEM((3, 256, COLUMNS), BF16),
            pltpu.VMEM((2, 2, 256, COLUMNS), BF16),
            pltpu.VMEM((2, 2, 256, COLUMNS), BF16),
            pltpu.SemaphoreType.DMA((COPIES,)),
            pltpu.SemaphoreType.DMA((COPIES,)),
        ],
        compiler_params=pltpu.CompilerParams(
            collective_id=0, has_side_effects=True, vmem_limit_bytes=32 * 2**20
        ),
        name="solve",
    )(dense, right_t)


def solution(mesh):
    in_specs = (
        P("leaf", None),
        P("leaf", "col", None, None, None),
        P("leaf", "col", None),
        P("leaf", "col", None),
        P("leaf", "col"),
    )
    out_specs = P(("leaf", "col"), None)
    return jax.shard_map(body, mesh=mesh, in_specs=in_specs, out_specs=out_specs, check_vma=False)
```

time: 318 us -> 57.6 us (0.18)
  waiting for transfers between devices: 166 us -> 0 us
  other arithmetic: 60.8 us -> 0 us
  Pallas kernels: 0 us -> 51.5 us
  local copies, waits for them, and re-layouts: 45.3 us -> 5.12 us
  matrix products: 19.7 us -> 0 us
  between operations: 14.3 us -> 0.68 us
  starting transfers between devices: 11.1 us -> 0 us
    ppermute x6 -> x0, waiting for transfers between devices: 132 us -> none  [from_partner(): lax.ppermute(x, axis, [(i, i ^ 1 << apart) for i in range(lax.axis_size(a...]
    scatter-add x2 -> x0, other arithmetic: 56.2 us -> none  [the longest x1 28.2 us: body(): terms = jnp.zeros((row_blocks, block_size, columns), jnp.float32).at[bloc...]
    pallas_call x0 -> x2, Pallas kernels: none -> 51.5 us  [the longest x1 43.1 us: body(): pl.pallas_call(solve_kernel, out_shape=jax.ShapeDtypeStruct((ROWS // 4, C...]
    reduce_scatter x1 -> x0, waiting for transfers between devices: 34.2 us -> none  [body(): lax.psum_scatter(terms, 'col', scatter_dimension=0, tiled=True)]
    mul x2 -> x0, local copies, waits for them, and re-layouts: 25.2 us -> none  [the longest x1 12.6 us: body(): products * alive_weight]
    dot_general x2 -> x0, matrix products: 19.7 us -> none  [the longest x1 9.85 us: body(): jnp.einsum('kab,kbc->kac', blocks, gathered, preferred_element_type=jnp.f...]
    gather x2 -> x0, local copies, waits for them, and re-layouts: 14.4 us -> none  [the longest x1 7.19 us: body(): picked = rhs_blocks[block_rows]]
    ppermute x6 -> x0, starting transfers between devices: 11.1 us -> none  [from_partner(): lax.ppermute(x, axis, [(i, i ^ 1 << apart) for i in range(lax.axis_size(a...]
  transfers between devices with their start and end apart: 7 -> 0, of which waited for: 7 -> 0; matrix products, arithmetic and copies ran while one was open for 0% -> 0% of each run, Pallas kernels for 0% -> 0%
where the time goes in v1:
time: 57.6 us; the launch traced here: 57.3 us
  Pallas kernels  51.5 us (89%)
  local copies, waits for them, and re-layouts  5.12 us (9%)
  between operations  0.68 us (1%)
    pallas_call x1, Pallas kernels, body(): pl.pallas_call(solve_kernel, out_shape=jax.ShapeDtypeStruct((ROWS // 4, C...  43.1 us
    pallas_call x1, Pallas kernels, body(): pl.pallas_call(build_kernel, out_shape=(jax.ShapeDtypeStruct((ROWS, WIDTH...  8.38 us
    unnamed x9, local copies, waits for them, and re-layouts  5.12 us

profile of v1, /device:TPU:1, one launch (start us, length us, event | category | flops | bytes accessed | tf_op | source)
XLA Modules:
  0.0 57.3 jit_solution(500046101292841608)
XLA Ops:
  0.7 0.0 copy-start
  0.7 1.9 %copy-done = bf16[1,1,96,128,128]{4,3,2,1,0:T(8,128)(2,1)S(1)} copy-done((bf16[1,1,96,128,128]{4,3,2,1,0:T(8,128)(2,1)S(1)}, bf16[1,1,96,128,128]{4,3,2,1,0:T(8,128)(2,1)}, u32[]{:S(2)}) %copy-start) | copy-done | bytes 3145752
  2.5 0.0 copy-start.1
  2.5 1.2 %copy-done.1 = bf16[2048,256]{1,0:T(8,128)(2,1)S(1)} copy-done((bf16[2048,256]{1,0:T(8,128)(2,1)S(1)}, bf16[2048,256]{1,0:T(8,128)(2,1)}, u32[]{:S(2)}) %copy-start.1) | copy-done | bytes 1048600
  3.8 0.0 copy-start.2
  3.8 0.7 %copy-done.2 = s32[1,1,96]{2,1,0:T(1,128)S(1)} copy-done((s32[1,1,96]{2,1,0:T(1,128)S(1)}, s32[1,1,96]{2,1,0:T(1,128)}, u32[]{:S(2)}) %copy-start.2) | copy-done | bytes 408
  4.4 0.0 copy-start.3
  4.4 0.7 %copy-done.3 = s32[1,1,96]{2,1,0:T(1,128)S(1)} copy-done((s32[1,1,96]{2,1,0:T(1,128)S(1)}, s32[1,1,96]{2,1,0:T(1,128)}, u32[]{:S(2)}) %copy-start.3) | copy-done | bytes 408
  5.1 8.4 %build_dense.1 = (bf16[2048,1792]{1,0:T(8,128)(2,1)S(1)}, bf16[256,2048]{1,0:T(8,128)(2,1)S(1)}) custom-call(s32[1,1,96]{2,1,0:T(1,128)S(1)} %copy-done.2, s32[1,1,96]{2,1,0:T(1,128)S(1)} %copy-done.3, s32[1,1]{1,0:T(1,128)S(6)} %copy.7.count_ref, bf16[2048,256]{1,0:T(8,128)(2,1)S(1)} %copy-done.1, bf16[1,1,96,128,128]{4,3,2,1,0:T(8,128)(2,1)S(1)} %copy-done), custom_call_target="tpu_custom_call" | custom-call | tf_op jit(solution)/shard_map/build_dense/pallas_call | solution.py:310
  13.5 43.1 %solve.1 = bf16[512,256]{1,0:T(8,128)(2,1)S(1)} custom-call(bf16[2048,1792]{1,0:T(8,128)(2,1)S(1)} %get-tuple-element.7.dense, bf16[256,2048]{1,0:T(8,128)(2,1)S(1)} %get-tuple-element.8.right_t), custom_call_target="tpu_custom_call" | custom-call | tf_op jit(solution)/shard_map/solve/pallas_call | solution.py:325
  56.6 0.7 %copy.8 = bf16[512,256]{1,0:T(8,128)(2,1)} copy(bf16[512,256]{1,0:T(8,128)(2,1)S(1)} %solve.1) | data formatting | bytes 524288
Async XLA Ops:
  0.7 1.9 %copy-start = (bf16[1,1,96,128,128]{4,3,2,1,0:T(8,128)(2,1)S(1)}, bf16[1,1,96,128,128]{4,3,2,1,0:T(8,128)(2,1)}, u32[]{:S(2)}) copy-start(bf16[1,1,96,128,128]{4,3,2,1,0:T(8,128)(2,1)} %blocks_hbm.1) | copy-start | bytes 9437188
  2.5 1.2 %copy-start.1 = (bf16[2048,256]{1,0:T(8,128)(2,1)S(1)}, bf16[2048,256]{1,0:T(8,128)(2,1)}, u32[]{:S(2)}) copy-start(bf16[2048,256]{1,0:T(8,128)(2,1)} %right_hbm.1) | copy-start | bytes 3145732
  3.8 0.7 %copy-start.2 = (s32[1,1,96]{2,1,0:T(1,128)S(1)}, s32[1,1,96]{2,1,0:T(1,128)}, u32[]{:S(2)}) copy-start(s32[1,1,96]{2,1,0:T(1,128)} %row_ref.1) | copy-start | bytes 1156
  4.4 0.7 %copy-start.3 = (s32[1,1,96]{2,1,0:T(1,128)S(1)}, s32[1,1,96]{2,1,0:T(1,128)}, u32[]{:S(2)}) copy-start(s32[1,1,96]{2,1,0:T(1,128)} %col_ref.1) | copy-start | bytes 1156

commit v2 on v1

v2 whole, which is shorter than its diff:
```python
import jax
import jax.numpy as jnp
from jax import lax
from jax.experimental import pallas as pl
from jax.experimental.pallas import tpu as pltpu
from jax.sharding import PartitionSpec as P

BLOCK = 128
ROW_BLOCKS = 16
LIST_LEN = 96
COLUMNS = 256
SLOTS = 14
ROWS = ROW_BLOCKS * BLOCK
WIDTH = SLOTS * BLOCK
Z = 8
X = 4
HALF = COLUMNS // 2
MESH = pl.DeviceIdType.MESH
GROUPS = 8
PER_GROUP = LIST_LEN // GROUPS
F32 = jnp.float32
BF16 = jnp.bfloat16


def build_kernel(row_hbm, col_hbm, count_ref, blocks_hbm, dense, block_buf, extra, row_ref, col_ref, seen, sems):
    lists = []
    for n, (source, target) in enumerate(((row_hbm, row_ref), (col_hbm, col_ref))):
        lists.append(pltpu.make_async_copy(source, target, sems.at[GROUPS + n]))
        lists[-1].start()
    fetches = []
    for g in range(GROUPS):
        part = pl.ds(g * PER_GROUP, PER_GROUP)
        fetches.append(pltpu.make_async_copy(blocks_hbm.at[0, 0, part], block_buf.at[part], sems.at[g]))
        fetches[-1].start()

    @pl.loop(0, ROW_BLOCKS)
    def _(i):
        for c in range(SLOTS):
            seen[i * SLOTS + c] = -1

    @pl.loop(0, ROWS // 64)
    def _(i):
        dense[pl.ds(pl.multiple_of(i * 64, 64), 64), :] = jnp.zeros((64, WIDTH), BF16)

    for c in lists:
        c.wait()
    count = count_ref[0, 0]
    used = jnp.int32(0)
    for g in range(GROUPS):
        fetches[g].wait()

        def add_block(k, used):
            r = row_ref[0, 0, k]
            c = col_ref[0, 0, k]
            place = r * SLOTS + c
            state = seen[place]
            rows = pl.ds(pl.multiple_of(r * BLOCK, BLOCK), BLOCK)
            cols = pl.ds(pl.multiple_of(c * BLOCK, BLOCK), BLOCK)

            @pl.when(state == -1)
            def _():
                dense[rows, cols] = block_buf[k]
                seen[place] = -2

            @pl.when(state == -2)
            def _():
                total = dense[rows, cols].astype(F32) + block_buf[k].astype(F32)
                extra[used] = total
                dense[rows, cols] = total.astype(BF16)
                seen[place] = used

            @pl.when(state >= 0)
            def _():
                total = extra[state] + block_buf[k].astype(F32)
                extra[state] = total
                dense[rows, cols] = total.astype(BF16)

            return used + jnp.where(state == -2, 1, 0)

        used = lax.fori_loop(g * PER_GROUP, jnp.clip(count, g * PER_GROUP, (g + 1) * PER_GROUP), add_block, used)


def level_lanes(level, levels=1):
    start = (2 + (level - 1) * 2) * BLOCK
    return slice(start, start + levels * 2 * BLOCK)


TOP = level_lanes(5, 2)
LATE = level_lanes(4, 3)
EARLY = slice(0, LATE.start)
COPIES = 96


def dot_t(a, b):
    return lax.dot_general(a, b, (((1,), (1,)), ((), ())), preferred_element_type=F32)


def solve_kernel(
    dense, right, out,
    right_t, coarse, pair_in, own, one_in, z_out, z_in, quad_in, next_in, x_out, x_in,
    terms, y_far, y_far_in, y_out, y_in, send, recv,
):
    leaf = lax.axis_index("leaf")
    col = lax.axis_index("col")
    core = lax.rem(leaf, 2)
    z = lax.rem(leaf // 2, Z)
    x = leaf // (2 * Z)
    quad = z // 4
    in_quad = lax.rem(z, 4)

    def at(x_to, z_to, core_to):
        return ((x_to * Z + z_to) * 2 + core_to, col)

    partner = at(x, z, 1 - core)
    z_peer = [at(x, lax.rem(z + d, Z), core) for d in range(Z)]
    quad_peer = [at(x, quad * 4 + lax.rem(in_quad + d, 4), core) for d in range(4)]
    z_next = z + 1 - 2 * lax.rem(z, 2)
    x_peer = []
    for b in range(X):
        flip_0 = x + 1 - 2 * lax.rem(x, 2) if b & 1 else x
        high = flip_0 // 2
        flip_1 = flip_0 + 2 - 4 * high if b & 2 else flip_0
        x_peer.append(at(flip_1, z, core))
    up = (leaf, lax.rem(col + 1, 4))
    down = (leaf, lax.rem(col + 3, 4))

    barrier = pltpu.get_barrier_semaphore()
    peers = [z_peer[d] for d in (4, 3, 5, 2, 6, 1, 7)] + x_peer[1:] + [up, down, partner]
    for peer in peers:
        pl.semaphore_signal(barrier, inc=1, device_id=peer, device_id_type=MESH)

    started = []

    def copy(src, dst, to):
        n = len(started)
        c = pltpu.make_async_remote_copy(
            src_ref=src, dst_ref=dst, send_sem=send.at[n], recv_sem=recv.at[n], device_id=to, device_id_type=MESH
        )
        c.start()
        started.append(c)
        return c

    def wait_all(copies):
        for c in copies:
            c.wait_recv()

    mine = pl.ds(pl.multiple_of(core * HALF, HALF), HALF)
    other = pl.ds(pl.multiple_of((1 - core) * HALF, HALF), HALF)
    chunk = pl.ds(pl.multiple_of(core * HALF + z * 16, 16), 16)
    quad_rows = pl.ds(pl.multiple_of(core * HALF + in_quad * 32, 32), 32)
    one, two, three, four = (level_lanes(level) for level in (1, 2, 3, 4))

    def partial(lanes):
        own[:, lanes] = lax.dot_general(
            right_t[...], dense[:, lanes], (((1,), (0,)), ((), ())), preferred_element_type=F32
        )

    def pair_send(lanes):
        return copy(own.at[other, lanes], pair_in.at[:, lanes], partner)

    def pair_sum(pair, lanes):
        pair.wait_recv()
        total = own[mine, lanes] + pair_in[:, lanes]
        own[mine, lanes] = total
        z_out[:, lanes] = total.astype(BF16)

    def ring_send(lanes):
        copies = []
        for d in (4, 3, 5, 2, 6, 1, 7):
            rows = pl.ds(pl.multiple_of(lax.rem(z + d, Z) * 16, 16), 16)
            copies.append(copy(z_out.at[rows, lanes], z_in.at[d, :, lanes], z_peer[d]))
        return copies

    def ring_sum(copies, lanes):
        wait_all(copies)
        total = own[chunk, lanes]
        for d in range(1, Z):
            total += z_in[d, :, lanes].astype(F32)
        return total

    def ring_share(lanes):
        return [copy(coarse.at[chunk, lanes], coarse.at[chunk, lanes], z_peer[d]) for d in (4, 3, 5, 2, 6, 1, 7)]

    def give(lanes):
        return copy(coarse.at[mine, lanes], coarse.at[mine, lanes], partner)

    @pl.loop(0, ROW_BLOCKS)
    def _(i):
        rows = pl.ds(pl.multiple_of(i * BLOCK, BLOCK), BLOCK)
        right_t[:, rows] = right[rows, :].T

    partial(TOP)
    pl.semaphore_wait(barrier, len(peers))
    top_pair = pair_send(TOP)
    partial(four)
    four_pair = pair_send(four)
    pair_sum(top_pair, TOP)
    top_ring = ring_send(TOP)
    pair_sum(four_pair, four)
    four_ring = ring_send(four)
    partial(three)
    three_pair = pair_send(three)
    partial(two)
    two_pair = pair_send(two)
    pair_sum(three_pair, three)
    three_quad = []
    for d in (2, 1, 3):
        rows = pl.ds(pl.multiple_of(lax.rem(in_quad + d, 4) * 32, 32), 32)
        three_quad.append(copy(z_out.at[rows, three], quad_in.at[d], quad_peer[d]))
    pair_sum(two_pair, two)
    two_next = copy(z_out.at[:, two], next_in, at(x, z_next, core))
    partial(slice(0, one.stop))
    one_pair = copy(own.at[:, one], one_in, partner)
    coarse[:, 0:one.start] = own[:, 0:one.start].astype(BF16)

    x_out[...] = ring_sum(top_ring, TOP)
    six = slice(2 * BLOCK, 4 * BLOCK)
    x_copies = [
        copy(x_out.at[:, six], x_in.at[2, :, six], x_peer[2]),
        copy(x_out, x_in.at[1], x_peer[1]),
        copy(x_out.at[:, six], x_in.at[3, :, six], x_peer[3]),
    ]

    coarse[chunk, four] = ring_sum(four_ring, four).astype(BF16)
    four_share = ring_share(four)
    wait_all(three_quad)
    total = own[quad_rows, three]
    for d in range(1, 4):
        total += quad_in[d].astype(F32)
    coarse[quad_rows, three] = total.astype(BF16)
    three_share = [copy(coarse.at[quad_rows, three], coarse.at[quad_rows, three], quad_peer[d]) for d in (2, 1, 3)]

    wait_all(x_copies)
    coarse[chunk, TOP.start:TOP.start + 2 * BLOCK] = (x_out[:, 0:2 * BLOCK] + x_in[1, :, 0:2 * BLOCK]).astype(BF16)
    coarse[chunk, TOP.start + 2 * BLOCK:TOP.stop] = (
        (x_out[:, six] + x_in[1, :, six]) + (x_in[2, :, six] + x_in[3, :, six])
    ).astype(BF16)
    top_share = ring_share(TOP)

    two_next.wait_recv()
    coarse[mine, two] = (own[mine, two] + next_in[...].astype(F32)).astype(BF16)
    two_give = give(two)
    one_pair.wait_recv()
    coarse[:, one] = (own[:, one] + one_in[...]).astype(BF16)
    wait_all(three_share)
    three_give = give(three)
    wait_all([two_give, three_give])

    @pl.loop(0, ROWS // 256)
    def _(i):
        rows = pl.ds(pl.multiple_of(i * 256, 256), 256)
        terms[rows, :] = dot_t(dense[rows, EARLY], coarse[:, EARLY])

    wait_all(four_share)
    four_give = give(four)
    wait_all(top_share)
    top_give = give(TOP)
    wait_all([four_give, top_give])

    def finish(quarter, half):
        rows = pl.ds(pl.multiple_of(quarter * 512 + half * 256, 256), 256)
        return terms[rows, :] + dot_t(dense[rows, LATE], coarse[:, LATE])

    far = lax.rem(col + 2, 4)
    above = lax.rem(col + 1, 4)
    below = lax.rem(col + 3, 4)
    far_copies = []
    for way, to in ((0, up), (1, down)):
        y_far[way] = finish(far, way).astype(BF16)
        for piece in range(2):
            rows = pl.ds(piece * BLOCK, BLOCK)
            far_copies.append(copy(y_far.at[way, rows], y_far_in.at[way, rows], to))
    y_out[0, 1] = finish(above, 1).astype(BF16)
    up_direct = copy(y_out.at[0, 1], y_in.at[0, 1], up)
    y_out[1, 0] = finish(below, 0).astype(BF16)
    down_direct = copy(y_out.at[1, 0], y_in.at[1, 0], down)
    passing = (finish(above, 0), finish(below, 1))
    for way, quarter in ((0, above), (1, below)):
        rows = pl.ds(pl.multiple_of(quarter * 512 + way * 256, 256), 256)
        terms[rows, :] = passing[way]
    last = []
    for piece in range(2):
        for way, quarter, to in ((0, above, up), (1, below, down)):
            far_copies[way * 2 + piece].wait_recv()
            rows = pl.ds(piece * BLOCK, BLOCK)
            from_terms = pl.ds(pl.multiple_of(quarter * 512 + way * 256 + piece * BLOCK, BLOCK), BLOCK)
            y_out[way, way, rows] = (terms[from_terms, :] + y_far_in[way, rows].astype(F32)).astype(BF16)
            last.append(copy(y_out.at[way, way, rows], y_in.at[way, way, rows], to))
    for half in range(2):
        rows = pl.ds(pl.multiple_of(col * 512 + half * 256, 256), 256)
        terms[rows, :] = finish(col, half)
    wait_all([up_direct, down_direct] + last)
    for half in range(2):
        rows = pl.ds(pl.multiple_of(col * 512 + half * 256, 256), 256)
        total = terms[rows, :] + (y_in[0, half].astype(F32) + y_in[1, half].astype(F32))
        out[half * 256:(half + 1) * 256, :] = total.astype(BF16)
    for c in started:
        c.wait_send()


def stay(array):
    return pltpu.with_memory_space_constraint(array, pltpu.HBM)


def body(right_side, x_blocks, row_ids, col_ids, counts):
    vmem = pl.BlockSpec(memory_space=pltpu.VMEM)
    hbm = pl.BlockSpec(memory_space=pltpu.HBM)
    dense = pl.pallas_call(
        build_kernel,
        out_shape=jax.ShapeDtypeStruct((ROWS, WIDTH), BF16),
        in_specs=[hbm, hbm, pl.BlockSpec(memory_space=pltpu.SMEM), hbm],
        out_specs=vmem,
        scratch_shapes=[
            pltpu.VMEM((LIST_LEN, BLOCK, BLOCK), BF16),
            pltpu.VMEM((LIST_LEN // 2, BLOCK, BLOCK), F32),
            pltpu.SMEM((1, 1, LIST_LEN), jnp.int32),
            pltpu.SMEM((1, 1, LIST_LEN), jnp.int32),
            pltpu.SMEM((ROW_BLOCKS * SLOTS,), jnp.int32),
            pltpu.SemaphoreType.DMA((GROUPS + 2,)),
        ],
        compiler_params=pltpu.CompilerParams(vmem_limit_bytes=24 * 2**20),
        name="build_dense",
    )(stay(row_ids), stay(col_ids), counts, stay(x_blocks))
    return pl.pallas_call(
        solve_kernel,
        out_shape=jax.ShapeDtypeStruct((ROWS // 4, COLUMNS), BF16),
        in_specs=[vmem, vmem],
        out_specs=vmem,
        scratch_shapes=[
            pltpu.VMEM((COLUMNS, ROWS), BF16),
            pltpu.VMEM((COLUMNS, WIDTH), BF16),
            pltpu.VMEM((HALF, WIDTH), F32),
            pltpu.VMEM((COLUMNS, WIDTH), F32),
            pltpu.VMEM((COLUMNS, 2 * BLOCK), F32),
            pltpu.VMEM((HALF, WIDTH), BF16),
            pltpu.VMEM((Z, 16, WIDTH), BF16),
            pltpu.VMEM((4, 32, 2 * BLOCK), BF16),
            pltpu.VMEM((HALF, 2 * BLOCK), BF16),
            pltpu.VMEM((16, 4 * BLOCK), F32),
            pltpu.VMEM((X, 16, 4 * BLOCK), F32),
            pltpu.VMEM((ROWS, COLUMNS), F32),
            pltpu.VMEM((2, 256, COLUMNS), BF16),
            pltpu.VMEM((2, 256, COLUMNS), BF16),
            pltpu.VMEM((2, 2, 256, COLUMNS), BF16),
            pltpu.VMEM((2, 2, 256, COLUMNS), BF16),
            pltpu.SemaphoreType.DMA((COPIES,)),
            pltpu.SemaphoreType.DMA((COPIES,)),
        ],
        compiler_params=pltpu.CompilerParams(
            collective_id=0, has_side_effects=True, vmem_limit_bytes=32 * 2**20
        ),
        name="solve",
    )(dense, right_side)


def solution(mesh):
    in_specs = (
        P("leaf", None),
        P("leaf", "col", None, None, None),
        P("leaf", "col", None),
        P("leaf", "col", None),
        P("leaf", "col"),
    )
    out_specs = P(("leaf", "col"), None)
    return jax.shard_map(body, mesh=mesh, in_specs=in_specs, out_specs=out_specs, check_vma=False)
```

time: 57.6 us -> 46.4 us (0.81); the launches traced: 57.3 us -> 45.5 us
  Pallas kernels: 51.5 us -> 44 us
  local copies, waits for them, and re-layouts: 5.12 us -> 0.71 us
    pallas_call x1, Pallas kernels: 8.38 us -> 3.48 us  [body(): pl.pallas_call(build_kernel, out_shape=jax.ShapeDtypeStruct((ROWS, WIDTH)...]
    unnamed x9 -> x3, local copies, waits for them, and re-layouts: 5.12 us -> 0.71 us
    pallas_call x1, Pallas kernels: 43.1 us -> 40.6 us  [body(): pl.pallas_call(solve_kernel, out_shape=jax.ShapeDtypeStruct((ROWS // 4, C...]
where the time goes in v2:
time: 46.4 us; the launch traced here: 45.5 us
  Pallas kernels  44 us (95%)
  between operations  0.77 us (2%)
  local copies, waits for them, and re-layouts  0.71 us (2%)
    pallas_call x1, Pallas kernels, body(): pl.pallas_call(solve_kernel, out_shape=jax.ShapeDtypeStruct((ROWS // 4, C...  40.6 us
    pallas_call x1, Pallas kernels, body(): pl.pallas_call(build_kernel, out_shape=jax.ShapeDtypeStruct((ROWS, WIDTH)...  3.48 us

profile of v2, /device:TPU:1, one launch (start us, length us, event | category | flops | bytes accessed | tf_op | source)
XLA Modules:
  0.0 45.5 jit_solution(13176218662171275513)
XLA Ops:
  0.0 0.0 copy-start
  0.7 3.5 %build_dense.1.dense = bf16[2048,1792]{1,0:T(8,128)(2,1)S(1)} custom-call(s32[1,1,96]{2,1,0:T(1,128)} %row_hbm.1, s32[1,1,96]{2,1,0:T(1,128)} %col_hbm.1, s32[1,1]{1,0:T(1,128)S(6)} %copy.7.count_ref, bf16[1,1,96,128,128]{4,3,2,1,0:T(8,128)(2,1)} %blocks_hbm.1), custom_call_target="tpu_custom_call" | custom-call | tf_op jit(solution)/shard_map/build_dense/pallas_call | solution.py:308
  4.2 0.0 copy-done
  4.2 40.6 %solve.1 = bf16[512,256]{1,0:T(8,128)(2,1)S(1)} custom-call(bf16[2048,1792]{1,0:T(8,128)(2,1)S(1)} %build_dense.1.dense, bf16[2048,256]{1,0:T(8,128)(2,1)S(1)} %copy-done), custom_call_target="tpu_custom_call" | custom-call | tf_op jit(solution)/shard_map/solve/pallas_call | solution.py:324
  44.8 0.7 %copy.8 = bf16[512,256]{1,0:T(8,128)(2,1)} copy(bf16[512,256]{1,0:T(8,128)(2,1)S(1)} %solve.1) | data formatting | bytes 524288
Async XLA Ops:
  0.0 4.2 %copy-start = (bf16[2048,256]{1,0:T(8,128)(2,1)S(1)}, bf16[2048,256]{1,0:T(8,128)(2,1)}, u32[]{:S(2)}) copy-start(bf16[2048,256]{1,0:T(8,128)(2,1)} %right.1) | copy-start | bytes 3145732

commit v3 on v2

v3 whole, which is shorter than its diff:
```python
import jax
import jax.numpy as jnp
from jax import lax
from jax.experimental import pallas as pl
from jax.experimental.pallas import tpu as pltpu
from jax.sharding import PartitionSpec as P

BLOCK = 128
ROW_BLOCKS = 16
LIST_LEN = 96
COLUMNS = 256
SLOTS = 14
ROWS = ROW_BLOCKS * BLOCK
WIDTH = SLOTS * BLOCK
Z = 8
X = 4
HALF = COLUMNS // 2
MESH = pl.DeviceIdType.MESH
GROUPS = 8
PER_GROUP = LIST_LEN // GROUPS
F32 = jnp.float32
BF16 = jnp.bfloat16


def lane_block(slot):
    level = slot // 2
    side = lax.rem(slot, 2)
    late = 8 + side * 3 + (level - 4)
    mid = 4 + side * 2 + (level - 2)
    return jnp.where(slot >= 8, late, jnp.where(slot >= 4, mid, slot))


def build_kernel(row_hbm, col_hbm, count_ref, blocks_hbm, dense, block_buf, extra, row_ref, col_ref, seen, sems):
    lists = []
    for n, (source, target) in enumerate(((row_hbm, row_ref), (col_hbm, col_ref))):
        lists.append(pltpu.make_async_copy(source, target, sems.at[GROUPS + n]))
        lists[-1].start()
    fetches = []
    for g in range(GROUPS):
        part = pl.ds(g * PER_GROUP, PER_GROUP)
        fetches.append(pltpu.make_async_copy(blocks_hbm.at[0, 0, part], block_buf.at[part], sems.at[g]))
        fetches[-1].start()

    @pl.loop(0, ROW_BLOCKS)
    def _(i):
        for c in range(SLOTS):
            seen[i * SLOTS + c] = -1

    @pl.loop(0, ROWS // 64)
    def _(i):
        dense[pl.ds(pl.multiple_of(i * 64, 64), 64), :] = jnp.zeros((64, WIDTH), BF16)

    for c in lists:
        c.wait()
    count = count_ref[0, 0]
    used = jnp.int32(0)
    for g in range(GROUPS):
        fetches[g].wait()

        def add_block(k, used):
            r = row_ref[0, 0, k]
            c = lane_block(col_ref[0, 0, k])
            place = r * SLOTS + c
            state = seen[place]
            rows = pl.ds(pl.multiple_of(r * BLOCK, BLOCK), BLOCK)
            cols = pl.ds(pl.multiple_of(c * BLOCK, BLOCK), BLOCK)

            @pl.when(state == -1)
            def _():
                dense[rows, cols] = block_buf[k]
                seen[place] = -2

            @pl.when(state == -2)
            def _():
                total = dense[rows, cols].astype(F32) + block_buf[k].astype(F32)
                extra[used] = total
                dense[rows, cols] = total.astype(BF16)
                seen[place] = used

            @pl.when(state >= 0)
            def _():
                total = extra[state] + block_buf[k].astype(F32)
                extra[state] = total
                dense[rows, cols] = total.astype(BF16)

            return used + jnp.where(state == -2, 1, 0)

        used = lax.fori_loop(g * PER_GROUP, jnp.clip(count, g * PER_GROUP, (g + 1) * PER_GROUP), add_block, used)


INNER = slice(0, 2 * BLOCK)
ONE = slice(2 * BLOCK, 4 * BLOCK)
MID = slice(4 * BLOCK, 8 * BLOCK)
LATE = slice(8 * BLOCK, 14 * BLOCK)
RING_ORDER = (4, 3, 5, 2, 6, 1, 7)
COPIES = 80


def dot_t(a, b):
    return lax.dot_general(a, b, (((1,), (1,)), ((), ())), preferred_element_type=F32)


def solve_kernel(
    dense, right, out,
    right_t, coarse, own, late_in, mid_in, one_in, late_out, mid_out, ring_in, quad_in, next_in, x_out, x_in,
    terms, y_far, y_far_in, y_out, y_in, send, recv,
):
    leaf = lax.axis_index("leaf")
    col = lax.axis_index("col")
    core = lax.rem(leaf, 2)
    z = lax.rem(leaf // 2, Z)
    x = leaf // (2 * Z)
    quad = z // 4
    in_quad = lax.rem(z, 4)

    def at(x_to, z_to, core_to):
        return ((x_to * Z + z_to) * 2 + core_to, col)

    partner = at(x, z, 1 - core)
    z_peer = [at(x, lax.rem(z + d, Z), core) for d in range(Z)]
    quad_peer = [at(x, quad * 4 + lax.rem(in_quad + d, 4), core) for d in range(4)]
    z_next = at(x, z + 1 - 2 * lax.rem(z, 2), core)
    x_peer = []
    for b in range(X):
        flip_0 = x + 1 - 2 * lax.rem(x, 2) if b & 1 else x
        high = flip_0 // 2
        flip_1 = flip_0 + 2 - 4 * high if b & 2 else flip_0
        x_peer.append(at(flip_1, z, core))
    up = (leaf, lax.rem(col + 1, 4))
    down = (leaf, lax.rem(col + 3, 4))

    barrier = pltpu.get_barrier_semaphore()
    peers = [z_peer[d] for d in RING_ORDER] + x_peer[1:] + [up, down, partner]
    for peer in peers:
        pl.semaphore_signal(barrier, inc=1, device_id=peer, device_id_type=MESH)

    started = []

    def copy(src, dst, to):
        n = len(started)
        c = pltpu.make_async_remote_copy(
            src_ref=src, dst_ref=dst, send_sem=send.at[n], recv_sem=recv.at[n], device_id=to, device_id_type=MESH
        )
        c.start()
        started.append(c)
        return c

    def wait_all(copies):
        for c in copies:
            c.wait_recv()

    late_mine = pl.ds(pl.multiple_of(LATE.start + core * 384, BLOCK), 384)
    late_other = pl.ds(pl.multiple_of(LATE.start + (1 - core) * 384, BLOCK), 384)
    mid_mine = pl.ds(pl.multiple_of(MID.start + core * 256, BLOCK), 256)
    mid_other = pl.ds(pl.multiple_of(MID.start + (1 - core) * 256, BLOCK), 256)
    two_mine = pl.ds(pl.multiple_of(MID.start + core * 256, BLOCK), BLOCK)
    three_mine = pl.ds(pl.multiple_of(MID.start + core * 256 + BLOCK, BLOCK), BLOCK)
    four_mine = pl.ds(pl.multiple_of(LATE.start + core * 384, BLOCK), BLOCK)
    five_mine = pl.ds(pl.multiple_of(LATE.start + core * 384 + BLOCK, BLOCK), BLOCK)
    six_mine = pl.ds(pl.multiple_of(LATE.start + core * 384 + 2 * BLOCK, BLOCK), BLOCK)
    part_rows = [pl.ds(p * HALF, HALF) for p in range(2)]
    chunk = [pl.ds(pl.multiple_of(p * HALF + z * 16, 16), 16) for p in range(2)]
    quad_chunk = [pl.ds(pl.multiple_of(p * HALF + in_quad * 32, 32), 32) for p in range(2)]

    def partial(lanes):
        own[:, lanes] = lax.dot_general(
            right_t[...], dense[:, lanes], (((1,), (0,)), ((), ())), preferred_element_type=F32
        )

    @pl.loop(0, ROW_BLOCKS)
    def _(i):
        rows = pl.ds(pl.multiple_of(i * BLOCK, BLOCK), BLOCK)
        right_t[:, rows] = right[rows, :].T

    partial(LATE)
    pl.semaphore_wait(barrier, len(peers))
    late_pair = [copy(own.at[part_rows[p], late_other], late_in.at[part_rows[p]], partner) for p in range(2)]
    partial(MID)
    mid_pair = [copy(own.at[part_rows[p], mid_other], mid_in.at[part_rows[p]], partner) for p in range(2)]

    late_ring = []
    for p in range(2):
        late_pair[p].wait_recv()
        total = own[part_rows[p], late_mine] + late_in[part_rows[p]]
        own[part_rows[p], late_mine] = total
        late_out[part_rows[p]] = total.astype(BF16)
        ring = []
        for d in RING_ORDER:
            rows = pl.ds(pl.multiple_of(p * HALF + lax.rem(z + d, Z) * 16, 16), 16)
            ring.append(copy(late_out.at[rows], ring_in.at[p, d], z_peer[d]))
        late_ring.append(ring)
    mid_quad = []
    mid_next = []
    for p in range(2):
        mid_pair[p].wait_recv()
        total = own[part_rows[p], mid_mine] + mid_in[part_rows[p]]
        own[part_rows[p], mid_mine] = total
        mid_out[part_rows[p]] = total.astype(BF16)
        quads = []
        for d in (2, 1, 3):
            rows = pl.ds(pl.multiple_of(p * HALF + lax.rem(in_quad + d, 4) * 32, 32), 32)
            quads.append(copy(mid_out.at[rows, BLOCK:2 * BLOCK], quad_in.at[p, d], quad_peer[d]))
        mid_quad.append(quads)
        mid_next.append(copy(mid_out.at[part_rows[p], 0:BLOCK], next_in.at[part_rows[p]], z_next))
    partial(ONE)
    one_pair = copy(own.at[:, ONE], one_in, partner)
    partial(INNER)
    coarse[:, INNER] = own[:, INNER].astype(BF16)

    x_copies = []
    for p in range(2):
        wait_all(late_ring[p])
        total = own[chunk[p], late_mine]
        for d in range(1, Z):
            total += ring_in[p, d].astype(F32)
        coarse[chunk[p], four_mine] = total[:, 0:BLOCK].astype(BF16)
        x_out[p] = total[:, BLOCK:3 * BLOCK]
        x_copies.append([
            copy(x_out.at[p, :, BLOCK:2 * BLOCK], x_in.at[p, 2, :, BLOCK:2 * BLOCK], x_peer[2]),
            copy(x_out.at[p], x_in.at[p, 1], x_peer[1]),
            copy(x_out.at[p, :, BLOCK:2 * BLOCK], x_in.at[p, 3, :, BLOCK:2 * BLOCK], x_peer[3]),
        ])
    late_share = []
    mid_share = []
    for p in range(2):
        wait_all(mid_quad[p])
        total = own[quad_chunk[p], three_mine]
        for d in range(1, 4):
            total += quad_in[p, d].astype(F32)
        coarse[quad_chunk[p], three_mine] = total.astype(BF16)
        at_three = coarse.at[quad_chunk[p], three_mine]
        mid_share.append([copy(at_three, at_three, quad_peer[d]) for d in (2, 1, 3)])
        wait_all(x_copies[p])
        coarse[chunk[p], five_mine] = (x_out[p, :, 0:BLOCK] + x_in[p, 1, :, 0:BLOCK]).astype(BF16)
        coarse[chunk[p], six_mine] = (
            (x_out[p, :, BLOCK:2 * BLOCK] + x_in[p, 1, :, BLOCK:2 * BLOCK])
            + (x_in[p, 2, :, BLOCK:2 * BLOCK] + x_in[p, 3, :, BLOCK:2 * BLOCK])
        ).astype(BF16)
        at_late = coarse.at[chunk[p], late_mine]
        late_share.append([copy(at_late, at_late, z_peer[d]) for d in RING_ORDER])
    one_pair.wait_recv()
    coarse[:, ONE] = (own[:, ONE] + one_in[...]).astype(BF16)

    @pl.loop(0, ROWS // 256)
    def _(i):
        rows = pl.ds(pl.multiple_of(i * 256, 256), 256)
        terms[rows, :] = dot_t(dense[rows, 0:ONE.stop], coarse[:, 0:ONE.stop])


    def give_part(p):
        mid_next[p].wait_recv()
        coarse[part_rows[p], two_mine] = (own[part_rows[p], two_mine] + next_in[part_rows[p]].astype(F32)).astype(BF16)
        wait_all(mid_share[p])
        at_mid = coarse.at[part_rows[p], mid_mine]
        gives = [copy(at_mid, at_mid, partner)]
        wait_all(late_share[p])
        at_late = coarse.at[part_rows[p], late_mine]
        gives.append(copy(at_late, at_late, partner))
        wait_all(gives)

    def finish(p, quarter, half):
        rows = pl.ds(pl.multiple_of(quarter * 512 + half * 256, 256), 256)
        return terms[rows, p * HALF:(p + 1) * HALF] + dot_t(dense[rows, MID.start:WIDTH], coarse[part_rows[p], MID.start:WIDTH])

    far = lax.rem(col + 2, 4)
    nearby = (lax.rem(col + 1, 4), lax.rem(col + 3, 4))
    toward = (up, down)

    def send_far(p):
        copies = []
        for way in range(2):
            y_far[p, way] = finish(p, far, way).astype(BF16)
            copies.append(copy(y_far.at[p, way], y_far_in.at[p, way], toward[way]))
        return copies

    def send_direct(p):
        copies = []
        for way in range(2):
            y_out[p, way, 1 - way] = finish(p, nearby[way], 1 - way).astype(BF16)
            copies.append(copy(y_out.at[p, way, 1 - way], y_in.at[p, way, 1 - way], toward[way]))
        return copies

    def send_passed(p, far_copies):
        copies = []
        for way in range(2):
            value = finish(p, nearby[way], way)
            far_copies[way].wait_recv()
            y_out[p, way, way] = (value + y_far_in[p, way].astype(F32)).astype(BF16)
            copies.append(copy(y_out.at[p, way, way], y_in.at[p, way, way], toward[way]))
        return copies

    give_part(0)
    far_a = send_far(0)
    last = send_direct(0)
    give_part(1)
    far_b = send_far(1)
    last += send_passed(0, far_a)
    last += send_direct(1)
    last += send_passed(1, far_b)
    for p in range(2):
        for half in range(2):
            rows = pl.ds(pl.multiple_of(col * 512 + half * 256, 256), 256)
            terms[rows, p * HALF:(p + 1) * HALF] = finish(p, col, half)
    wait_all(last)
    for p in range(2):
        for half in range(2):
            rows = pl.ds(pl.multiple_of(col * 512 + half * 256, 256), 256)
            total = terms[rows, p * HALF:(p + 1) * HALF] + (y_in[p, 0, half].astype(F32) + y_in[p, 1, half].astype(F32))
            out[half * 256:(half + 1) * 256, p * HALF:(p + 1) * HALF] = total.astype(BF16)
    for c in started:
        c.wait_send()


def stay(array):
    return pltpu.with_memory_space_constraint(array, pltpu.HBM)


def body(right_side, x_blocks, row_ids, col_ids, counts):
    vmem = pl.BlockSpec(memory_space=pltpu.VMEM)
    hbm = pl.BlockSpec(memory_space=pltpu.HBM)
    dense = pl.pallas_call(
        build_kernel,
        out_shape=jax.ShapeDtypeStruct((ROWS, WIDTH), BF16),
        in_specs=[hbm, hbm, pl.BlockSpec(memory_space=pltpu.SMEM), hbm],
        out_specs=vmem,
        scratch_shapes=[
            pltpu.VMEM((LIST_LEN, BLOCK, BLOCK), BF16),
            pltpu.VMEM((LIST_LEN // 2, BLOCK, BLOCK), F32),
            pltpu.SMEM((1, 1, LIST_LEN), jnp.int32),
            pltpu.SMEM((1, 1, LIST_LEN), jnp.int32),
            pltpu.SMEM((ROW_BLOCKS * SLOTS,), jnp.int32),
            pltpu.SemaphoreType.DMA((GROUPS + 2,)),
        ],
        compiler_params=pltpu.CompilerParams(vmem_limit_bytes=24 * 2**20),
        name="build_dense",
    )(stay(row_ids), stay(col_ids), counts, stay(x_blocks))
    return pl.pallas_call(
        solve_kernel,
        out_shape=jax.ShapeDtypeStruct((ROWS // 4, COLUMNS), BF16),
        in_specs=[vmem, vmem],
        out_specs=vmem,
        scratch_shapes=[
            pltpu.VMEM((COLUMNS, ROWS), BF16),
            pltpu.VMEM((COLUMNS, WIDTH), BF16),
            pltpu.VMEM((COLUMNS, WIDTH), F32),
            pltpu.VMEM((COLUMNS, 3 * BLOCK), F32),
            pltpu.VMEM((COLUMNS, 2 * BLOCK), F32),
            pltpu.VMEM((COLUMNS, 2 * BLOCK), F32),
            pltpu.VMEM((COLUMNS, 3 * BLOCK), BF16),
            pltpu.VMEM((COLUMNS, 2 * BLOCK), BF16),
            pltpu.VMEM((2, Z, 16, 3 * BLOCK), BF16),
            pltpu.VMEM((2, 4, 32, BLOCK), BF16),
            pltpu.VMEM((COLUMNS, BLOCK), BF16),
            pltpu.VMEM((2, 16, 2 * BLOCK), F32),
            pltpu.VMEM((2, X, 16, 2 * BLOCK), F32),
            pltpu.VMEM((ROWS, COLUMNS), F32),
            pltpu.VMEM((2, 2, 256, HALF), BF16),
            pltpu.VMEM((2, 2, 256, HALF), BF16),
            pltpu.VMEM((2, 2, 2, 256, HALF), BF16),
            pltpu.VMEM((2, 2, 2, 256, HALF), BF16),
            pltpu.SemaphoreType.DMA((COPIES,)),
            pltpu.SemaphoreType.DMA((COPIES,)),
        ],
        compiler_params=pltpu.CompilerParams(
            collective_id=0, has_side_effects=True, vmem_limit_bytes=32 * 2**20
        ),
        name="solve",
    )(dense, right_side)


def solution(mesh):
    in_specs = (
        P("leaf", None),
        P("leaf", "col", None, None, None),
        P("leaf", "col", None),
        P("leaf", "col", None),
        P("leaf", "col"),
    )
    out_specs = P(("leaf", "col"), None)
    return jax.shard_map(body, mesh=mesh, in_specs=in_specs, out_specs=out_specs, check_vma=False)
```

time: 46.4 us -> 45.5 us (0.981); the launches traced: 45.5 us -> 45.5 us
  no operation moved by 1% of the time
where the time goes in v3:
time: 45.5 us
  Pallas kernels  44 us (97%)
  between operations  0.77 us (2%)
  local copies, waits for them, and re-layouts  0.71 us (2%)
    pallas_call x1, Pallas kernels, body(): pl.pallas_call(solve_kernel, out_shape=jax.ShapeDtypeStruct((ROWS // 4, C...  40.5 us
    pallas_call x1, Pallas kernels, body(): pl.pallas_call(build_kernel, out_shape=jax.ShapeDtypeStruct((ROWS, WIDTH)...  3.51 us

profile of v3, /device:TPU:1, one launch (start us, length us, event | category | flops | bytes accessed | tf_op | source)
XLA Modules:
  0.0 45.5 jit_solution(10623037593519230816)
XLA Ops:
  0.0 0.0 copy-start
  0.7 3.5 %build_dense.1.dense = bf16[2048,1792]{1,0:T(8,128)(2,1)S(1)} custom-call(s32[1,1,96]{2,1,0:T(1,128)} %row_hbm.1, s32[1,1,96]{2,1,0:T(1,128)} %col_hbm.1, s32[1,1]{1,0:T(1,128)S(6)} %copy.7.count_ref, bf16[1,1,96,128,128]{4,3,2,1,0:T(8,128)(2,1)} %blocks_hbm.1), custom_call_target="tpu_custom_call" | custom-call | tf_op jit(solution)/shard_map/build_dense/pallas_call | solution.py:321
  4.3 0.0 copy-done
  4.3 40.5 %solve.1 = bf16[512,256]{1,0:T(8,128)(2,1)S(1)} custom-call(bf16[2048,1792]{1,0:T(8,128)(2,1)S(1)} %build_dense.1.dense, bf16[2048,256]{1,0:T(8,128)(2,1)S(1)} %copy-done), custom_call_target="tpu_custom_call" | custom-call | tf_op jit(solution)/shard_map/solve/pallas_call | solution.py:337
  44.8 0.7 %copy.8 = bf16[512,256]{1,0:T(8,128)(2,1)} copy(bf16[512,256]{1,0:T(8,128)(2,1)S(1)} %solve.1) | data formatting | bytes 524288
Async XLA Ops:
  0.0 4.3 %copy-start = (bf16[2048,256]{1,0:T(8,128)(2,1)S(1)}, bf16[2048,256]{1,0:T(8,128)(2,1)}, u32[]{:S(2)}) copy-start(bf16[2048,256]{1,0:T(8,128)(2,1)} %right.1) | copy-start | bytes 3145732

commit v4 on v3

v4 whole, which is shorter than its diff:
```python
import jax
import jax.numpy as jnp
from jax import lax
from jax.experimental import pallas as pl
from jax.experimental.pallas import tpu as pltpu
from jax.sharding import PartitionSpec as P

BLOCK = 128
ROW_BLOCKS = 16
LIST_LEN = 96
COLUMNS = 256
SLOTS = 14
ROWS = ROW_BLOCKS * BLOCK
WIDTH = SLOTS * BLOCK
Z = 8
X = 4
HALF = COLUMNS // 2
MESH = pl.DeviceIdType.MESH
GROUPS = 8
PER_GROUP = LIST_LEN // GROUPS
F32 = jnp.float32
BF16 = jnp.bfloat16


def lane_block(slot):
    level = slot // 2
    side = lax.rem(slot, 2)
    late = 8 + side * 3 + (level - 4)
    mid = 4 + side * 2 + (level - 2)
    return jnp.where(slot >= 8, late, jnp.where(slot >= 4, mid, slot))


def build_kernel(
    row_hbm, col_hbm, count_ref, right_hbm, blocks_hbm, dense, right_t,
    right_buf, block_buf, extra, row_ref, col_ref, row_at, col_at, seen, slot_of, again, first, sems,
):
    lists = []
    for n, (source, target) in enumerate(((row_hbm, row_ref), (col_hbm, col_ref))):
        lists.append(pltpu.make_async_copy(source, target, sems.at[GROUPS + n]))
        lists[-1].start()
    fetch_right = pltpu.make_async_copy(right_hbm, right_buf, sems.at[GROUPS + 2])
    fetch_right.start()
    fetches = []
    for g in range(GROUPS):
        part = pl.ds(g * PER_GROUP, PER_GROUP)
        fetches.append(pltpu.make_async_copy(blocks_hbm.at[0, 0, part], block_buf.at[part], sems.at[g]))
        fetches[-1].start()

    @pl.loop(0, ROW_BLOCKS)
    def _(i):
        for c in range(SLOTS):
            seen[i * SLOTS + c] = -1

    @pl.loop(0, ROWS // 64)
    def _(i):
        dense[pl.ds(pl.multiple_of(i * 64, 64), 64), :] = jnp.zeros((64, WIDTH), BF16)

    for c in lists:
        c.wait()
    count = count_ref[0, 0]

    def place_block(k, repeats):
        r = row_ref[0, 0, k]
        c = lane_block(col_ref[0, 0, k])
        row_at[k] = r * BLOCK
        col_at[k] = c * BLOCK
        slot_of[k] = -1
        place = r * SLOTS + c
        earlier = seen[place]
        again[repeats] = k
        first[repeats] = earlier
        seen[place] = jnp.where(earlier >= 0, earlier, k)
        return repeats + jnp.where(earlier >= 0, 1, 0)

    repeats = lax.fori_loop(0, count, place_block, jnp.int32(0))
    fetch_right.wait()

    @pl.loop(0, ROW_BLOCKS)
    def _(i):
        rows = pl.ds(pl.multiple_of(i * BLOCK, BLOCK), BLOCK)
        right_t[:, rows] = right_buf[rows, :].T

    def target(k):
        return pl.ds(pl.multiple_of(row_at[k], BLOCK), BLOCK), pl.ds(pl.multiple_of(col_at[k], BLOCK), BLOCK)

    for g in range(GROUPS):
        fetches[g].wait()

        @pl.when(g * PER_GROUP < count)
        def _():
            @pl.loop(0, PER_GROUP // 4)
            def _(i):
                for n in range(4):
                    k = jnp.minimum(g * PER_GROUP + i * 4 + n, count - 1)
                    rows, cols = target(k)
                    dense[rows, cols] = block_buf[k]

    def add_again(i, used):
        k = again[i]
        f = first[i]
        rows, cols = target(k)
        slot = slot_of[f]

        @pl.when(slot < 0)
        def _():
            total = block_buf[f].astype(F32) + block_buf[k].astype(F32)
            extra[used] = total
            dense[rows, cols] = total.astype(BF16)
            slot_of[f] = used

        @pl.when(slot >= 0)
        def _():
            total = extra[slot] + block_buf[k].astype(F32)
            extra[slot] = total
            dense[rows, cols] = total.astype(BF16)

        return used + jnp.where(slot < 0, 1, 0)

    lax.fori_loop(0, repeats, add_again, jnp.int32(0))


INNER = slice(0, 2 * BLOCK)
ONE = slice(2 * BLOCK, 4 * BLOCK)
MID = slice(4 * BLOCK, 8 * BLOCK)
LATE = slice(8 * BLOCK, 14 * BLOCK)
RING_ORDER = (4, 3, 5, 2, 6, 1, 7)
COPIES = 80


def dot_t(a, b):
    return lax.dot_general(a, b, (((1,), (1,)), ((), ())), preferred_element_type=F32)


def solve_kernel(
    dense, right_t, out,
    coarse_low, coarse_mid, coarse_late, own_one, own_mid, own_late, late_send, late_in, mid_in, one_in, late_out, mid_out,
    ring_in, quad_in, next_in, x_out, x_in,
    terms, y_far, y_far_in, y_out, y_in, send, recv,
):
    leaf = lax.axis_index("leaf")
    col = lax.axis_index("col")
    core = lax.rem(leaf, 2)
    z = lax.rem(leaf // 2, Z)
    x = leaf // (2 * Z)
    quad = z // 4
    in_quad = lax.rem(z, 4)

    def at(x_to, z_to, core_to):
        return ((x_to * Z + z_to) * 2 + core_to, col)

    partner = at(x, z, 1 - core)
    z_peer = [at(x, lax.rem(z + d, Z), core) for d in range(Z)]
    quad_peer = [at(x, quad * 4 + lax.rem(in_quad + d, 4), core) for d in range(4)]
    z_next = at(x, z + 1 - 2 * lax.rem(z, 2), core)
    x_peer = []
    for b in range(X):
        flip_0 = x + 1 - 2 * lax.rem(x, 2) if b & 1 else x
        high = flip_0 // 2
        flip_1 = flip_0 + 2 - 4 * high if b & 2 else flip_0
        x_peer.append(at(flip_1, z, core))
    up = (leaf, lax.rem(col + 1, 4))
    down = (leaf, lax.rem(col + 3, 4))

    barrier = pltpu.get_barrier_semaphore()
    peers = [z_peer[d] for d in RING_ORDER] + x_peer[1:] + [up, down, partner]
    for peer in peers:
        pl.semaphore_signal(barrier, inc=1, device_id=peer, device_id_type=MESH)

    started = []

    def copy(src, dst, to):
        n = len(started)
        c = pltpu.make_async_remote_copy(
            src_ref=src, dst_ref=dst, send_sem=send.at[n], recv_sem=recv.at[n], device_id=to, device_id_type=MESH
        )
        c.start()
        started.append(c)
        return c

    def wait_all(copies):
        for c in copies:
            c.wait_recv()

    part_rows = [pl.ds(p * HALF, HALF) for p in range(2)]
    chunk = [pl.ds(pl.multiple_of(p * HALF + z * 16, 16), 16) for p in range(2)]
    quad_chunk = [pl.ds(pl.multiple_of(p * HALF + in_quad * 32, 32), 32) for p in range(2)]

    def partial(lanes):
        return lax.dot_general(right_t[...], dense[:, lanes], (((1,), (0,)), ((), ())), preferred_element_type=F32)

    def late_lanes(side):
        return pl.ds(pl.multiple_of(LATE.start + side * 384, BLOCK), 384)

    late_send[...] = partial(late_lanes(1 - core))
    pl.semaphore_wait(barrier, len(peers))
    late_pair = [copy(late_send.at[part_rows[p]], late_in.at[part_rows[p]], partner) for p in range(2)]
    own_late[...] = partial(late_lanes(core))

    late_ring = []
    for p in range(2):
        late_pair[p].wait_recv()
        total = own_late[part_rows[p]] + late_in[part_rows[p]]
        own_late[part_rows[p]] = total
        late_out[part_rows[p]] = total.astype(BF16)
        ring = []
        for d in RING_ORDER:
            rows = pl.ds(pl.multiple_of(p * HALF + lax.rem(z + d, Z) * 16, 16), 16)
            ring.append(copy(late_out.at[rows], ring_in.at[p, d], z_peer[d]))
        late_ring.append(ring)
    value = partial(MID)
    for side in range(2):
        for n in range(2):
            own_mid[side, n] = value[:, (side * 2 + n) * BLOCK:(side * 2 + n + 1) * BLOCK]
    mid_pair = [copy(own_mid.at[1 - core, :, part_rows[p]], mid_in.at[:, part_rows[p]], partner) for p in range(2)]
    mid_quad = []
    mid_next = []
    for p in range(2):
        mid_pair[p].wait_recv()
        total = own_mid[core, :, part_rows[p]] + mid_in[:, part_rows[p]]
        own_mid[core, :, part_rows[p]] = total
        mid_out[:, part_rows[p]] = total.astype(BF16)
        quads = []
        for d in (2, 1, 3):
            rows = pl.ds(pl.multiple_of(p * HALF + lax.rem(in_quad + d, 4) * 32, 32), 32)
            quads.append(copy(mid_out.at[1, rows], quad_in.at[p, d], quad_peer[d]))
        mid_quad.append(quads)
        mid_next.append(copy(mid_out.at[0, part_rows[p]], next_in.at[part_rows[p]], z_next))
    own_one[...] = partial(ONE)
    one_pair = copy(own_one, one_in, partner)
    coarse_low[:, INNER] = partial(INNER).astype(BF16)

    x_copies = []
    for p in range(2):
        wait_all(late_ring[p])
        total = own_late[chunk[p]]
        for d in range(1, Z):
            total += ring_in[p, d].astype(F32)
        coarse_late[core, chunk[p], 0:BLOCK] = total[:, 0:BLOCK].astype(BF16)
        x_out[p] = total[:, BLOCK:3 * BLOCK]
        x_copies.append([
            copy(x_out.at[p, :, BLOCK:2 * BLOCK], x_in.at[p, 2, :, BLOCK:2 * BLOCK], x_peer[2]),
            copy(x_out.at[p], x_in.at[p, 1], x_peer[1]),
            copy(x_out.at[p, :, BLOCK:2 * BLOCK], x_in.at[p, 3, :, BLOCK:2 * BLOCK], x_peer[3]),
        ])
    late_share = []
    mid_share = []
    for p in range(2):
        wait_all(mid_quad[p])
        total = own_mid[core, 1, quad_chunk[p]]
        for d in range(1, 4):
            total += quad_in[p, d].astype(F32)
        coarse_mid[core, 1, quad_chunk[p]] = total.astype(BF16)
        at_three = coarse_mid.at[core, 1, quad_chunk[p]]
        mid_share.append([copy(at_three, at_three, quad_peer[d]) for d in (2, 1, 3)])
        wait_all(x_copies[p])
        coarse_late[core, chunk[p], BLOCK:2 * BLOCK] = (x_out[p, :, 0:BLOCK] + x_in[p, 1, :, 0:BLOCK]).astype(BF16)
        coarse_late[core, chunk[p], 2 * BLOCK:3 * BLOCK] = (
            (x_out[p, :, BLOCK:2 * BLOCK] + x_in[p, 1, :, BLOCK:2 * BLOCK])
            + (x_in[p, 2, :, BLOCK:2 * BLOCK] + x_in[p, 3, :, BLOCK:2 * BLOCK])
        ).astype(BF16)
        at_late = coarse_late.at[core, chunk[p]]
        late_share.append([copy(at_late, at_late, z_peer[d]) for d in RING_ORDER])
    one_pair.wait_recv()
    coarse_low[:, ONE] = (own_one[...] + one_in[...]).astype(BF16)

    @pl.loop(0, ROWS // 256)
    def _(i):
        rows = pl.ds(pl.multiple_of(i * 256, 256), 256)
        terms[rows, :] = dot_t(dense[rows, 0:ONE.stop], coarse_low[...])


    def give_part(p):
        mid_next[p].wait_recv()
        coarse_mid[core, 0, part_rows[p]] = (own_mid[core, 0, part_rows[p]] + next_in[part_rows[p]].astype(F32)).astype(BF16)
        wait_all(mid_share[p])
        at_mid = coarse_mid.at[core, :, part_rows[p]]
        gives = [copy(at_mid, at_mid, partner)]
        wait_all(late_share[p])
        at_late = coarse_late.at[core, part_rows[p]]
        gives.append(copy(at_late, at_late, partner))
        wait_all(gives)

    def finish(p, quarter, half):
        rows = pl.ds(pl.multiple_of(quarter * 512 + half * 256, 256), 256)
        pieces = [coarse_mid[side, n, part_rows[p]] for side in range(2) for n in range(2)]
        pieces += [coarse_late[side, part_rows[p]] for side in range(2)]
        coarse = jnp.concatenate(pieces, axis=1)
        return terms[rows, p * HALF:(p + 1) * HALF] + dot_t(dense[rows, MID.start:WIDTH], coarse)

    far = lax.rem(col + 2, 4)
    nearby = (lax.rem(col + 1, 4), lax.rem(col + 3, 4))
    toward = (up, down)

    def send_far(p):
        copies = []
        for way in range(2):
            y_far[p, way] = finish(p, far, way).astype(BF16)
            copies.append(copy(y_far.at[p, way], y_far_in.at[p, way], toward[way]))
        return copies

    def send_direct(p):
        copies = []
        for way in range(2):
            y_out[p, way, 1 - way] = finish(p, nearby[way], 1 - way).astype(BF16)
            copies.append(copy(y_out.at[p, way, 1 - way], y_in.at[p, way, 1 - way], toward[way]))
        return copies

    def send_passed(p, far_copies):
        copies = []
        for way in range(2):
            value = finish(p, nearby[way], way)
            far_copies[way].wait_recv()
            y_out[p, way, way] = (value + y_far_in[p, way].astype(F32)).astype(BF16)
            copies.append(copy(y_out.at[p, way, way], y_in.at[p, way, way], toward[way]))
        return copies

    give_part(0)
    far_a = send_far(0)
    last = send_direct(0)
    give_part(1)
    far_b = send_far(1)
    last += send_direct(1)
    last += send_passed(0, far_a)
    last += send_passed(1, far_b)
    for p in range(2):
        for half in range(2):
            rows = pl.ds(pl.multiple_of(col * 512 + half * 256, 256), 256)
            terms[rows, p * HALF:(p + 1) * HALF] = finish(p, col, half)
    wait_all(last)
    for p in range(2):
        for half in range(2):
            rows = pl.ds(pl.multiple_of(col * 512 + half * 256, 256), 256)
            total = terms[rows, p * HALF:(p + 1) * HALF] + (y_in[p, 0, half].astype(F32) + y_in[p, 1, half].astype(F32))
            out[half * 256:(half + 1) * 256, p * HALF:(p + 1) * HALF] = total.astype(BF16)
    for c in started:
        c.wait_send()


def stay(array):
    return pltpu.with_memory_space_constraint(array, pltpu.HBM)


def body(right_side, x_blocks, row_ids, col_ids, counts):
    vmem = pl.BlockSpec(memory_space=pltpu.VMEM)
    hbm = pl.BlockSpec(memory_space=pltpu.HBM)
    dense, right_t = pl.pallas_call(
        build_kernel,
        out_shape=(jax.ShapeDtypeStruct((ROWS, WIDTH), BF16), jax.ShapeDtypeStruct((COLUMNS, ROWS), BF16)),
        in_specs=[hbm, hbm, pl.BlockSpec(memory_space=pltpu.SMEM), hbm, hbm],
        out_specs=(vmem, vmem),
        scratch_shapes=[
            pltpu.VMEM((ROWS, COLUMNS), BF16),
            pltpu.VMEM((LIST_LEN, BLOCK, BLOCK), BF16),
            pltpu.VMEM((LIST_LEN // 2, BLOCK, BLOCK), F32),
            pltpu.SMEM((1, 1, LIST_LEN), jnp.int32),
            pltpu.SMEM((1, 1, LIST_LEN), jnp.int32),
            pltpu.SMEM((LIST_LEN,), jnp.int32),
            pltpu.SMEM((LIST_LEN,), jnp.int32),
            pltpu.SMEM((ROW_BLOCKS * SLOTS,), jnp.int32),
            pltpu.SMEM((LIST_LEN,), jnp.int32),
            pltpu.SMEM((LIST_LEN,), jnp.int32),
            pltpu.SMEM((LIST_LEN,), jnp.int32),
            pltpu.SemaphoreType.DMA((GROUPS + 3,)),
        ],
        compiler_params=pltpu.CompilerParams(vmem_limit_bytes=24 * 2**20),
        name="build_dense",
    )(stay(row_ids), stay(col_ids), counts, stay(right_side), stay(x_blocks))
    return pl.pallas_call(
        solve_kernel,
        out_shape=jax.ShapeDtypeStruct((ROWS // 4, COLUMNS), BF16),
        in_specs=[vmem, vmem],
        out_specs=vmem,
        scratch_shapes=[
            pltpu.VMEM((COLUMNS, 4 * BLOCK), BF16),
            pltpu.VMEM((2, 2, COLUMNS, BLOCK), BF16),
            pltpu.VMEM((2, COLUMNS, 3 * BLOCK), BF16),
            pltpu.VMEM((COLUMNS, 2 * BLOCK), F32),
            pltpu.VMEM((2, 2, COLUMNS, BLOCK), F32),
            pltpu.VMEM((COLUMNS, 3 * BLOCK), F32),
            pltpu.VMEM((COLUMNS, 3 * BLOCK), F32),
            pltpu.VMEM((COLUMNS, 3 * BLOCK), F32),
            pltpu.VMEM((2, COLUMNS, BLOCK), F32),
            pltpu.VMEM((COLUMNS, 2 * BLOCK), F32),
            pltpu.VMEM((COLUMNS, 3 * BLOCK), BF16),
            pltpu.VMEM((2, COLUMNS, BLOCK), BF16),
            pltpu.VMEM((2, Z, 16, 3 * BLOCK), BF16),
            pltpu.VMEM((2, 4, 32, BLOCK), BF16),
            pltpu.VMEM((COLUMNS, BLOCK), BF16),
            pltpu.VMEM((2, 16, 2 * BLOCK), F32),
            pltpu.VMEM((2, X, 16, 2 * BLOCK), F32),
            pltpu.VMEM((ROWS, COLUMNS), F32),
            pltpu.VMEM((2, 2, 256, HALF), BF16),
            pltpu.VMEM((2, 2, 256, HALF), BF16),
            pltpu.VMEM((2, 2, 2, 256, HALF), BF16),
            pltpu.VMEM((2, 2, 2, 256, HALF), BF16),
            pltpu.SemaphoreType.DMA((COPIES,)),
            pltpu.SemaphoreType.DMA((COPIES,)),
        ],
        compiler_params=pltpu.CompilerParams(
            collective_id=0, has_side_effects=True, vmem_limit_bytes=32 * 2**20
        ),
        name="solve",
    )(dense, right_t)


def solution(mesh):
    in_specs = (
        P("leaf", None),
        P("leaf", "col", None, None, None),
        P("leaf", "col", None),
        P("leaf", "col", None),
        P("leaf", "col"),
    )
    out_specs = P(("leaf", "col"), None)
    return jax.shard_map(body, mesh=mesh, in_specs=in_specs, out_specs=out_specs, check_vma=False)
```

time: 45.5 us -> 45.8 us (level)
    pallas_call x1, Pallas kernels: 3.51 us -> 5.66 us  [body(): pl.pallas_call(build_kernel, out_shape=(jax.ShapeDtypeStruct((ROWS, WIDTH...]
    pallas_call x1, Pallas kernels: 40.5 us -> 38.7 us  [body(): pl.pallas_call(solve_kernel, out_shape=jax.ShapeDtypeStruct((ROWS // 4, C...]
where the time goes in v4:
time: 45.8 us
  Pallas kernels  44.4 us (97%)
  local copies, waits for them, and re-layouts  0.71 us (2%)
  between operations  0.67 us (1%)
    pallas_call x1, Pallas kernels, body(): pl.pallas_call(solve_kernel, out_shape=jax.ShapeDtypeStruct((ROWS // 4, C...  38.7 us
    pallas_call x1, Pallas kernels, body(): pl.pallas_call(build_kernel, out_shape=(jax.ShapeDtypeStruct((ROWS, WIDTH...  5.66 us

profile of v4, /device:TPU:1, one launch (start us, length us, event | category | flops | bytes accessed | tf_op | source)
XLA Modules:
  0.0 45.8 jit_solution(17654965560660170189)
XLA Ops:
  0.7 5.7 %build_dense.1 = (bf16[2048,1792]{1,0:T(8,128)(2,1)S(1)}, bf16[256,2048]{1,0:T(8,128)(2,1)S(1)}) custom-call(s32[1,1,96]{2,1,0:T(1,128)} %row_hbm.1, s32[1,1,96]{2,1,0:T(1,128)} %col_hbm.1, s32[1,1]{1,0:T(1,128)S(6)} %copy.7.count_ref, bf16[2048,256]{1,0:T(8,128)(2,1)} %right_hbm.1, bf16[1,1,96,128,128]{4,3,2,1,0:T(8,128)(2,1)} %blocks_hbm.1), custom_call_target="tpu_custom_call" | custom-call | tf_op jit(solution)/shard_map/build_dense/pallas_call | solution.py:346
  6.3 38.7 %solve.1 = bf16[512,256]{1,0:T(8,128)(2,1)S(1)} custom-call(bf16[2048,1792]{1,0:T(8,128)(2,1)S(1)} %get-tuple-element.7.dense, bf16[256,2048]{1,0:T(8,128)(2,1)S(1)} %get-tuple-element.8.right_t), custom_call_target="tpu_custom_call" | custom-call | tf_op jit(solution)/shard_map/solve/pallas_call | solution.py:368
  45.1 0.7 %copy.8 = bf16[512,256]{1,0:T(8,128)(2,1)} copy(bf16[512,256]{1,0:T(8,128)(2,1)S(1)} %solve.1) | data formatting | bytes 524288

commit v5 on v4

--- a/solution.py
+++ b/solution.py
@@ -22,34 +22,41 @@
 BF16 = jnp.bfloat16
 
 
-def lane_block(slot):
-    level = slot // 2
-    side = lax.rem(slot, 2)
-    late = 8 + side * 3 + (level - 4)
-    mid = 4 + side * 2 + (level - 2)
-    return jnp.where(slot >= 8, late, jnp.where(slot >= 4, mid, slot))
+def lane_of(slot):
+    level, side = slot // 2, slot % 2
+    if slot >= 8:
+        return (8 + side * 3 + level - 4) * BLOCK
+    if slot >= 4:
+        return (4 + side * 2 + level - 2) * BLOCK
+    return slot * BLOCK
 
 
 def build_kernel(
-    row_hbm, col_hbm, count_ref, right_hbm, blocks_hbm, dense, right_t,
-    right_buf, block_buf, extra, row_ref, col_ref, row_at, col_at, seen, slot_of, again, first, sems,
+    row_hbm, col_hbm, count_ref, blocks_hbm, dense, block_buf, extra, row_ref, col_ref, lanes, seen, slot_of, used, sems
 ):
     lists = []
     for n, (source, target) in enumerate(((row_hbm, row_ref), (col_hbm, col_ref))):
         lists.append(pltpu.make_async_copy(source, target, sems.at[GROUPS + n]))
         lists[-1].start()
-    fetch_right = pltpu.make_async_copy(right_hbm, right_buf, sems.at[GROUPS + 2])
-    fetch_right.start()
     fetches = []
     for g in range(GROUPS):
         part = pl.ds(g * PER_GROUP, PER_GROUP)
         fetches.append(pltpu.make_async_copy(blocks_hbm.at[0, 0, part], block_buf.at[part], sems.at[g]))
         fetches[-1].start()
 
+    used[0] = 0
+    for slot in range(SLOTS):
+        lanes[slot] = lane_of(slot)
+
     @pl.loop(0, ROW_BLOCKS)
     def _(i):
         for c in range(SLOTS):
             seen[i * SLOTS + c] = -1
+
+    @pl.loop(0, LIST_LEN // 16)
+    def _(i):
+        for n in range(16):
+            slot_of[i * 16 + n] = -1
 
     @pl.loop(0, ROWS // 64)
     def _(i):
@@ -58,65 +65,38 @@
     for c in lists:
         c.wait()
     count = count_ref[0, 0]
-
-    def place_block(k, repeats):
-        r = row_ref[0, 0, k]
-        c = lane_block(col_ref[0, 0, k])
-        row_at[k] = r * BLOCK
-        col_at[k] = c * BLOCK
-        slot_of[k] = -1
-        place = r * SLOTS + c
-        earlier = seen[place]
-        again[repeats] = k
-        first[repeats] = earlier
-        seen[place] = jnp.where(earlier >= 0, earlier, k)
-        return repeats + jnp.where(earlier >= 0, 1, 0)
-
-    repeats = lax.fori_loop(0, count, place_block, jnp.int32(0))
-    fetch_right.wait()
-
-    @pl.loop(0, ROW_BLOCKS)
-    def _(i):
-        rows = pl.ds(pl.multiple_of(i * BLOCK, BLOCK), BLOCK)
-        right_t[:, rows] = right_buf[rows, :].T
-
-    def target(k):
-        return pl.ds(pl.multiple_of(row_at[k], BLOCK), BLOCK), pl.ds(pl.multiple_of(col_at[k], BLOCK), BLOCK)
-
     for g in range(GROUPS):
         fetches[g].wait()
 
-        @pl.when(g * PER_GROUP < count)
-        def _():
-            @pl.loop(0, PER_GROUP // 4)
-            def _(i):
-                for n in range(4):
-                    k = jnp.minimum(g * PER_GROUP + i * 4 + n, count - 1)
-                    rows, cols = target(k)
-                    dense[rows, cols] = block_buf[k]
-
-    def add_again(i, used):
-        k = again[i]
-        f = first[i]
-        rows, cols = target(k)
-        slot = slot_of[f]
-
-        @pl.when(slot < 0)
-        def _():
-            total = block_buf[f].astype(F32) + block_buf[k].astype(F32)
-            extra[used] = total
-            dense[rows, cols] = total.astype(BF16)
-            slot_of[f] = used
-
-        @pl.when(slot >= 0)
-        def _():
-            total = extra[slot] + block_buf[k].astype(F32)
-            extra[slot] = total
-            dense[rows, cols] = total.astype(BF16)
-
-        return used + jnp.where(slot < 0, 1, 0)
-
-    lax.fori_loop(0, repeats, add_again, jnp.int32(0))
+        @pl.loop(g * PER_GROUP, jnp.clip(count, g * PER_GROUP, (g + 1) * PER_GROUP))
+        def _(k):
+            r = row_ref[0, 0, k]
+            c = col_ref[0, 0, k]
+            place = r * SLOTS + c
+            first = seen[place]
+            rows = pl.ds(pl.multiple_of(r * BLOCK, BLOCK), BLOCK)
+            cols = pl.ds(pl.multiple_of(lanes[c], BLOCK), BLOCK)
+            dense[rows, cols] = block_buf[k]
+            seen[place] = jnp.where(first < 0, k, first)
+
+            @pl.when(first >= 0)
+            def _():
+                slot = slot_of[first]
+
+                @pl.when(slot < 0)
+                def _():
+                    n = used[0]
+                    total = block_buf[first].astype(F32) + block_buf[k].astype(F32)
+                    extra[n] = total
+                    dense[rows, cols] = total.astype(BF16)
+                    slot_of[first] = n
+                    used[0] = n + 1
+
+                @pl.when(slot >= 0)
+                def _():
+                    total = extra[slot] + block_buf[k].astype(F32)
+                    extra[slot] = total
+                    dense[rows, cols] = total.astype(BF16)
 
 
 INNER = slice(0, 2 * BLOCK)
@@ -132,8 +112,8 @@
 
 
 def solve_kernel(
-    dense, right_t, out,
-    coarse_low, coarse_mid, coarse_late, own_one, own_mid, own_late, late_send, late_in, mid_in, one_in, late_out, mid_out,
+    dense, right, out,
+    right_t, coarse_low, coarse_mid, coarse_late, own_one, own_mid, own_late, late_send, late_in, mid_in, one_in, late_out, mid_out,
     ring_in, quad_in, next_in, x_out, x_in,
     terms, y_far, y_far_in, y_out, y_in, send, recv,
 ):
@@ -187,6 +167,11 @@
 
     def partial(lanes):
         return lax.dot_general(right_t[...], dense[:, lanes], (((1,), (0,)), ((), ())), preferred_element_type=F32)
+
+    @pl.loop(0, ROW_BLOCKS)
+    def _(i):
+        rows = pl.ds(pl.multiple_of(i * BLOCK, BLOCK), BLOCK)
+        right_t[:, rows] = right[rows, :].T
 
     def late_lanes(side):
         return pl.ds(pl.multiple_of(LATE.start + side * 384, BLOCK), 384)
@@ -343,34 +328,32 @@
 def body(right_side, x_blocks, row_ids, col_ids, counts):
     vmem = pl.BlockSpec(memory_space=pltpu.VMEM)
     hbm = pl.BlockSpec(memory_space=pltpu.HBM)
-    dense, right_t = pl.pallas_call(
+    dense = pl.pallas_call(
         build_kernel,
-        out_shape=(jax.ShapeDtypeStruct((ROWS, WIDTH), BF16), jax.ShapeDtypeStruct((COLUMNS, ROWS), BF16)),
-        in_specs=[hbm, hbm, pl.BlockSpec(memory_space=pltpu.SMEM), hbm, hbm],
-        out_specs=(vmem, vmem),
+        out_shape=jax.ShapeDtypeStruct((ROWS, WIDTH), BF16),
+        in_specs=[hbm, hbm, pl.BlockSpec(memory_space=pltpu.SMEM), hbm],
+        out_specs=vmem,
         scratch_shapes=[
-            pltpu.VMEM((ROWS, COLUMNS), BF16),
             pltpu.VMEM((LIST_LEN, BLOCK, BLOCK), BF16),
             pltpu.VMEM((LIST_LEN // 2, BLOCK, BLOCK), F32),
             pltpu.SMEM((1, 1, LIST_LEN), jnp.int32),
             pltpu.SMEM((1, 1, LIST_LEN), jnp.int32),
-            pltpu.SMEM((LIST_LEN,), jnp.int32),
-            pltpu.SMEM((LIST_LEN,), jnp.int32),
+            pltpu.SMEM((SLOTS,), jnp.int32),
             pltpu.SMEM((ROW_BLOCKS * SLOTS,), jnp.int32),
             pltpu.SMEM((LIST_LEN,), jnp.int32),
-            pltpu.SMEM((LIST_LEN,), jnp.int32),
-            pltpu.SMEM((LIST_LEN,), jnp.int32),
-            pltpu.SemaphoreType.DMA((GROUPS + 3,)),
+            pltpu.SMEM((1,), jnp.int32),
+            pltpu.SemaphoreType.DMA((GROUPS + 2,)),
         ],
         compiler_params=pltpu.CompilerParams(vmem_limit_bytes=24 * 2**20),
         name="build_dense",
-    )(stay(row_ids), stay(col_ids), counts, stay(right_side), stay(x_blocks))
+    )(stay(row_ids), stay(col_ids), counts, stay(x_blocks))
     return pl.pallas_call(
         solve_kernel,
         out_shape=jax.ShapeDtypeStruct((ROWS // 4, COLUMNS), BF16),
         in_specs=[vmem, vmem],
         out_specs=vmem,
         scratch_shapes=[
+            pltpu.VMEM((COLUMNS, ROWS), BF16),
             pltpu.VMEM((COLUMNS, 4 * BLOCK), BF16),
             pltpu.VMEM((2, 2, COLUMNS, BLOCK), BF16),
             pltpu.VMEM((2, COLUMNS, 3 * BLOCK), BF16),
@@ -400,7 +383,7 @@
             collective_id=0, has_side_effects=True, vmem_limit_bytes=32 * 2**20
         ),
         name="solve",
-    )(dense, right_t)
+    )(dense, right_side)
 
 
 def solution(mesh):

time: 45.8 us -> 43.2 us (0.943)
  Pallas kernels: 44.4 us -> 41.7 us
    pallas_call x1, Pallas kernels: 5.66 us -> 3.02 us  [body(): pl.pallas_call(build_kernel, out_shape=jax.ShapeDtypeStruct((ROWS, WIDTH)...]
where the time goes in v5:
time: 43.2 us
  Pallas kernels  41.7 us (97%)
  between operations  0.77 us (2%)
  local copies, waits for them, and re-layouts  0.71 us (2%)
    pallas_call x1, Pallas kernels, body(): pl.pallas_call(solve_kernel, out_shape=jax.ShapeDtypeStruct((ROWS // 4, C...  38.7 us
    pallas_call x1, Pallas kernels, body(): pl.pallas_call(build_kernel, out_shape=jax.ShapeDtypeStruct((ROWS, WIDTH)...  3.02 us

profile of v5, /device:TPU:1, one launch (start us, length us, event | category | flops | bytes accessed | tf_op | source)
XLA Modules:
  0.0 43.2 jit_solution(12703837517471360685)
XLA Ops:
  0.0 0.0 copy-start
  0.7 3.0 %build_dense.1.dense = bf16[2048,1792]{1,0:T(8,128)(2,1)S(1)} custom-call(s32[1,1,96]{2,1,0:T(1,128)} %row_hbm.1, s32[1,1,96]{2,1,0:T(1,128)} %col_hbm.1, s32[1,1]{1,0:T(1,128)S(6)} %copy.7.count_ref, bf16[1,1,96,128,128]{4,3,2,1,0:T(8,128)(2,1)} %blocks_hbm.1), custom_call_target="tpu_custom_call" | custom-call | tf_op jit(solution)/shard_map/build_dense/pallas_call | solution.py:331
  3.8 0.0 copy-done
  3.8 38.7 %solve.1 = bf16[512,256]{1,0:T(8,128)(2,1)S(1)} custom-call(bf16[2048,1792]{1,0:T(8,128)(2,1)S(1)} %build_dense.1.dense, bf16[2048,256]{1,0:T(8,128)(2,1)S(1)} %copy-done), custom_call_target="tpu_custom_call" | custom-call | tf_op jit(solution)/shard_map/solve/pallas_call | solution.py:350
  42.5 0.7 %copy.8 = bf16[512,256]{1,0:T(8,128)(2,1)} copy(bf16[512,256]{1,0:T(8,128)(2,1)S(1)} %solve.1) | data formatting | bytes 524288
Async XLA Ops:
  0.0 3.8 %copy-start = (bf16[2048,256]{1,0:T(8,128)(2,1)S(1)}, bf16[2048,256]{1,0:T(8,128)(2,1)}, u32[]{:S(2)}) copy-start(bf16[2048,256]{1,0:T(8,128)(2,1)} %right.1) | copy-start | bytes 3145732

commit v6 on v5

--- a/solution.py
+++ b/solution.py
@@ -104,7 +104,7 @@
 MID = slice(4 * BLOCK, 8 * BLOCK)
 LATE = slice(8 * BLOCK, 14 * BLOCK)
 RING_ORDER = (4, 3, 5, 2, 6, 1, 7)
-COPIES = 80
+COPIES = 112
 
 
 def dot_t(a, b):
@@ -113,8 +113,8 @@
 
 def solve_kernel(
     dense, right, out,
-    right_t, coarse_low, coarse_mid, coarse_late, own_one, own_mid, own_late, late_send, late_in, mid_in, one_in, late_out, mid_out,
-    ring_in, quad_in, next_in, x_out, x_in,
+    right_t, coarse_low, coarse_mid, coarse_four, coarse_top, own_one, own_mid, own_late, late_send, late_in, mid_in, one_in,
+    four_out, top_out, mid_out, four_in, top_in, quad_in, next_in, x_out, x_in,
     terms, y_far, y_far_in, y_out, y_in, send, recv,
 ):
     leaf = lax.axis_index("leaf")
@@ -168,10 +168,11 @@
     def partial(lanes):
         return lax.dot_general(right_t[...], dense[:, lanes], (((1,), (0,)), ((), ())), preferred_element_type=F32)
 
-    @pl.loop(0, ROW_BLOCKS)
-    def _(i):
-        rows = pl.ds(pl.multiple_of(i * BLOCK, BLOCK), BLOCK)
-        right_t[:, rows] = right[rows, :].T
+    square = (COLUMNS, COLUMNS)
+    identity = (lax.broadcasted_iota(jnp.int32, square, 0) == lax.broadcasted_iota(jnp.int32, square, 1)).astype(BF16)
+    for i in range(ROWS // COLUMNS):
+        rows = slice(i * COLUMNS, (i + 1) * COLUMNS)
+        right_t[:, rows] = dot_t(identity, right[rows, :]).astype(BF16)
 
     def late_lanes(side):
         return pl.ds(pl.multiple_of(LATE.start + side * 384, BLOCK), 384)
@@ -181,17 +182,22 @@
     late_pair = [copy(late_send.at[part_rows[p]], late_in.at[part_rows[p]], partner) for p in range(2)]
     own_late[...] = partial(late_lanes(core))
 
-    late_ring = []
+    def ring_send(p, source, target):
+        ring = []
+        for d in RING_ORDER:
+            rows = pl.ds(pl.multiple_of(p * HALF + lax.rem(z + d, Z) * 16, 16), 16)
+            ring.append(copy(source.at[rows], target.at[p, d], z_peer[d]))
+        return ring
+
+    top_ring = []
     for p in range(2):
         late_pair[p].wait_recv()
         total = own_late[part_rows[p]] + late_in[part_rows[p]]
         own_late[part_rows[p]] = total
-        late_out[part_rows[p]] = total.astype(BF16)
-        ring = []
-        for d in RING_ORDER:
-            rows = pl.ds(pl.multiple_of(p * HALF + lax.rem(z + d, Z) * 16, 16), 16)
-            ring.append(copy(late_out.at[rows], ring_in.at[p, d], z_peer[d]))
-        late_ring.append(ring)
+        four_out[part_rows[p]] = total[:, 0:BLOCK].astype(BF16)
+        top_out[part_rows[p]] = total[:, BLOCK:3 * BLOCK].astype(BF16)
+        top_ring.append(ring_send(p, top_out, top_in))
+    four_ring = [ring_send(p, four_out, four_in) for p in range(2)]
     value = partial(MID)
     for side in range(2):
         for n in range(2):
@@ -216,18 +222,26 @@
 
     x_copies = []
     for p in range(2):
-        wait_all(late_ring[p])
-        total = own_late[chunk[p]]
+        wait_all(top_ring[p])
+        total = own_late[chunk[p], BLOCK:3 * BLOCK]
         for d in range(1, Z):
-            total += ring_in[p, d].astype(F32)
-        coarse_late[core, chunk[p], 0:BLOCK] = total[:, 0:BLOCK].astype(BF16)
-        x_out[p] = total[:, BLOCK:3 * BLOCK]
+            total += top_in[p, d].astype(F32)
+        x_out[p] = total
         x_copies.append([
             copy(x_out.at[p, :, BLOCK:2 * BLOCK], x_in.at[p, 2, :, BLOCK:2 * BLOCK], x_peer[2]),
             copy(x_out.at[p], x_in.at[p, 1], x_peer[1]),
             copy(x_out.at[p, :, BLOCK:2 * BLOCK], x_in.at[p, 3, :, BLOCK:2 * BLOCK], x_peer[3]),
         ])
-    late_share = []
+    four_share = []
+    for p in range(2):
+        wait_all(four_ring[p])
+        total = own_late[chunk[p], 0:BLOCK]
+        for d in range(1, Z):
+            total += four_in[p, d].astype(F32)
+        coarse_four[core, chunk[p]] = total.astype(BF16)
+        at_four = coarse_four.at[core, chunk[p]]
+        four_share.append([copy(at_four, at_four, z_peer[d]) for d in RING_ORDER])
+    top_share = []
     mid_share = []
     for p in range(2):
         wait_all(mid_quad[p])
@@ -238,13 +252,13 @@
         at_three = coarse_mid.at[core, 1, quad_chunk[p]]
         mid_share.append([copy(at_three, at_three, quad_peer[d]) for d in (2, 1, 3)])
         wait_all(x_copies[p])
-        coarse_late[core, chunk[p], BLOCK:2 * BLOCK] = (x_out[p, :, 0:BLOCK] + x_in[p, 1, :, 0:BLOCK]).astype(BF16)
-        coarse_late[core, chunk[p], 2 * BLOCK:3 * BLOCK] = (
+        coarse_top[core, chunk[p], 0:BLOCK] = (x_out[p, :, 0:BLOCK] + x_in[p, 1, :, 0:BLOCK]).astype(BF16)
+        coarse_top[core, chunk[p], BLOCK:2 * BLOCK] = (
             (x_out[p, :, BLOCK:2 * BLOCK] + x_in[p, 1, :, BLOCK:2 * BLOCK])
             + (x_in[p, 2, :, BLOCK:2 * BLOCK] + x_in[p, 3, :, BLOCK:2 * BLOCK])
         ).astype(BF16)
-        at_late = coarse_late.at[core, chunk[p]]
-        late_share.append([copy(at_late, at_late, z_peer[d]) for d in RING_ORDER])
+        at_top = coarse_top.at[core, chunk[p]]
+        top_share.append([copy(at_top, at_top, z_peer[d]) for d in RING_ORDER])
     one_pair.wait_recv()
     coarse_low[:, ONE] = (own_one[...] + one_in[...]).astype(BF16)
 
@@ -260,15 +274,19 @@
         wait_all(mid_share[p])
         at_mid = coarse_mid.at[core, :, part_rows[p]]
         gives = [copy(at_mid, at_mid, partner)]
-        wait_all(late_share[p])
-        at_late = coarse_late.at[core, part_rows[p]]
-        gives.append(copy(at_late, at_late, partner))
+        wait_all(four_share[p])
+        at_four = coarse_four.at[core, part_rows[p]]
+        gives.append(copy(at_four, at_four, partner))
+        wait_all(top_share[p])
+        at_top = coarse_top.at[core, part_rows[p]]
+        gives.append(copy(at_top, at_top, partner))
         wait_all(gives)
 
     def finish(p, quarter, half):
         rows = pl.ds(pl.multiple_of(quarter * 512 + half * 256, 256), 256)
         pieces = [coarse_mid[side, n, part_rows[p]] for side in range(2) for n in range(2)]
-        pieces += [coarse_late[side, part_rows[p]] for side in range(2)]
+        for side in range(2):
+            pieces += [coarse_four[side, part_rows[p]], coarse_top[side, part_rows[p]]]
         coarse = jnp.concatenate(pieces, axis=1)
         return terms[rows, p * HALF:(p + 1) * HALF] + dot_t(dense[rows, MID.start:WIDTH], coarse)
 
@@ -356,7 +374,8 @@
             pltpu.VMEM((COLUMNS, ROWS), BF16),
             pltpu.VMEM((COLUMNS, 4 * BLOCK), BF16),
             pltpu.VMEM((2, 2, COLUMNS, BLOCK), BF16),
-            pltpu.VMEM((2, COLUMNS, 3 * BLOCK), BF16),
+            pltpu.VMEM((2, COLUMNS, BLOCK), BF16),
+            pltpu.VMEM((2, COLUMNS, 2 * BLOCK), BF16),
             pltpu.VMEM((COLUMNS, 2 * BLOCK), F32),
             pltpu.VMEM((2, 2, COLUMNS, BLOCK), F32),
             pltpu.VMEM((COLUMNS, 3 * BLOCK), F32),
@@ -364,9 +383,11 @@
             pltpu.VMEM((COLUMNS, 3 * BLOCK), F32),
             pltpu.VMEM((2, COLUMNS, BLOCK), F32),
             pltpu.VMEM((COLUMNS, 2 * BLOCK), F32),
-            pltpu.VMEM((COLUMNS, 3 * BLOCK), BF16),
+            pltpu.VMEM((COLUMNS, BLOCK), BF16),
+            pltpu.VMEM((COLUMNS, 2 * BLOCK), BF16),
             pltpu.VMEM((2, COLUMNS, BLOCK), BF16),
-            pltpu.VMEM((2, Z, 16, 3 * BLOCK), BF16),
+            pltpu.VMEM((2, Z, 16, BLOCK), BF16),
+            pltpu.VMEM((2, Z, 16, 2 * BLOCK), BF16),
             pltpu.VMEM((2, 4, 32, BLOCK), BF16),
             pltpu.VMEM((COLUMNS, BLOCK), BF16),
             pltpu.VMEM((2, 16, 2 * BLOCK), F32),

time: 43.2 us -> 43.5 us (level)
    pallas_call x1, Pallas kernels: 38.7 us -> 39.2 us  [body(): pl.pallas_call(solve_kernel, out_shape=jax.ShapeDtypeStruct((ROWS // 4, C...]
where the time goes in v6:
time: 43.5 us; the launch traced here: 43.4 us
  Pallas kernels  41.9 us (96%)
  between operations  0.77 us (2%)
  local copies, waits for them, and re-layouts  0.71 us (2%)
    pallas_call x1, Pallas kernels, body(): pl.pallas_call(solve_kernel, out_shape=jax.ShapeDtypeStruct((ROWS // 4, C...  39.2 us
    pallas_call x1, Pallas kernels, body(): pl.pallas_call(build_kernel, out_shape=jax.ShapeDtypeStruct((ROWS, WIDTH)...  2.71 us

profile of v6, /device:TPU:1, one launch (start us, length us, event | category | flops | bytes accessed | tf_op | source)
XLA Modules:
  0.0 43.4 jit_solution(2151940371783160073)
XLA Ops:
  0.0 0.0 copy-start
  0.7 2.7 %build_dense.1.dense = bf16[2048,1792]{1,0:T(8,128)(2,1)S(1)} custom-call(s32[1,1,96]{2,1,0:T(1,128)} %row_hbm.1, s32[1,1,96]{2,1,0:T(1,128)} %col_hbm.1, s32[1,1]{1,0:T(1,128)S(6)} %copy.7.count_ref, bf16[1,1,96,128,128]{4,3,2,1,0:T(8,128)(2,1)} %blocks_hbm.1), custom_call_target="tpu_custom_call" | custom-call | tf_op jit(solution)/shard_map/build_dense/pallas_call | solution.py:349
  3.5 0.0 copy-done
  3.5 39.2 %solve.1 = bf16[512,256]{1,0:T(8,128)(2,1)S(1)} custom-call(bf16[2048,1792]{1,0:T(8,128)(2,1)S(1)} %build_dense.1.dense, bf16[2048,256]{1,0:T(8,128)(2,1)S(1)} %copy-done), custom_call_target="tpu_custom_call" | custom-call | tf_op jit(solution)/shard_map/solve/pallas_call | solution.py:368
  42.7 0.7 %copy.8 = bf16[512,256]{1,0:T(8,128)(2,1)} copy(bf16[512,256]{1,0:T(8,128)(2,1)S(1)} %solve.1) | data formatting | bytes 524288
Async XLA Ops:
  0.0 3.5 %copy-start = (bf16[2048,256]{1,0:T(8,128)(2,1)S(1)}, bf16[2048,256]{1,0:T(8,128)(2,1)}, u32[]{:S(2)}) copy-start(bf16[2048,256]{1,0:T(8,128)(2,1)} %right.1) | copy-start | bytes 3145732

commit v7 on v6

--- a/solution.py
+++ b/solution.py
@@ -233,6 +233,8 @@
             copy(x_out.at[p, :, BLOCK:2 * BLOCK], x_in.at[p, 3, :, BLOCK:2 * BLOCK], x_peer[3]),
         ])
     four_share = []
+    top_share = []
+    mid_share = []
     for p in range(2):
         wait_all(four_ring[p])
         total = own_late[chunk[p], 0:BLOCK]
@@ -241,9 +243,6 @@
         coarse_four[core, chunk[p]] = total.astype(BF16)
         at_four = coarse_four.at[core, chunk[p]]
         four_share.append([copy(at_four, at_four, z_peer[d]) for d in RING_ORDER])
-    top_share = []
-    mid_share = []
-    for p in range(2):
         wait_all(mid_quad[p])
         total = own_mid[core, 1, quad_chunk[p]]
         for d in range(1, 4):
@@ -269,17 +268,18 @@
 
 
     def give_part(p):
-        mid_next[p].wait_recv()
-        coarse_mid[core, 0, part_rows[p]] = (own_mid[core, 0, part_rows[p]] + next_in[part_rows[p]].astype(F32)).astype(BF16)
-        wait_all(mid_share[p])
-        at_mid = coarse_mid.at[core, :, part_rows[p]]
-        gives = [copy(at_mid, at_mid, partner)]
+        gives = []
         wait_all(four_share[p])
         at_four = coarse_four.at[core, part_rows[p]]
         gives.append(copy(at_four, at_four, partner))
         wait_all(top_share[p])
         at_top = coarse_top.at[core, part_rows[p]]
         gives.append(copy(at_top, at_top, partner))
+        mid_next[p].wait_recv()
+        coarse_mid[core, 0, part_rows[p]] = (own_mid[core, 0, part_rows[p]] + next_in[part_rows[p]].astype(F32)).astype(BF16)
+        wait_all(mid_share[p])
+        at_mid = coarse_mid.at[core, :, part_rows[p]]
+        gives.append(copy(at_mid, at_mid, partner))
         wait_all(gives)
 
     def finish(p, quarter, half):

time: 43.5 us -> 43.3 us (level)
  no operation moved by 1% of the time
where the time goes in v7:
time: 43.3 us; the launch traced here: 43.4 us
  Pallas kernels  41.9 us (97%)
  between operations  0.77 us (2%)
  local copies, waits for them, and re-layouts  0.71 us (2%)
    pallas_call x1, Pallas kernels, body(): pl.pallas_call(solve_kernel, out_shape=jax.ShapeDtypeStruct((ROWS // 4, C...  39.2 us
    pallas_call x1, Pallas kernels, body(): pl.pallas_call(build_kernel, out_shape=jax.ShapeDtypeStruct((ROWS, WIDTH)...  2.69 us

profile of v7, /device:TPU:1, one launch (start us, length us, event | category | flops | bytes accessed | tf_op | source)
XLA Modules:
  0.0 43.4 jit_solution(10837025589837278794)
XLA Ops:
  0.0 0.0 copy-start
  0.7 2.7 %build_dense.1.dense = bf16[2048,1792]{1,0:T(8,128)(2,1)S(1)} custom-call(s32[1,1,96]{2,1,0:T(1,128)} %row_hbm.1, s32[1,1,96]{2,1,0:T(1,128)} %col_hbm.1, s32[1,1]{1,0:T(1,128)S(6)} %copy.7.count_ref, bf16[1,1,96,128,128]{4,3,2,1,0:T(8,128)(2,1)} %blocks_hbm.1), custom_call_target="tpu_custom_call" | custom-call | tf_op jit(solution)/shard_map/build_dense/pallas_call | solution.py:349
  3.4 0.0 copy-done
  3.4 39.2 %solve.1 = bf16[512,256]{1,0:T(8,128)(2,1)S(1)} custom-call(bf16[2048,1792]{1,0:T(8,128)(2,1)S(1)} %build_dense.1.dense, bf16[2048,256]{1,0:T(8,128)(2,1)S(1)} %copy-done), custom_call_target="tpu_custom_call" | custom-call | tf_op jit(solution)/shard_map/solve/pallas_call | solution.py:368
  42.7 0.7 %copy.8 = bf16[512,256]{1,0:T(8,128)(2,1)} copy(bf16[512,256]{1,0:T(8,128)(2,1)S(1)} %solve.1) | data formatting | bytes 524288
Async XLA Ops:
  0.0 3.4 %copy-start = (bf16[2048,256]{1,0:T(8,128)(2,1)S(1)}, bf16[2048,256]{1,0:T(8,128)(2,1)}, u32[]{:S(2)}) copy-start(bf16[2048,256]{1,0:T(8,128)(2,1)} %right.1) | copy-start | bytes 3145732

commit v8 on v6

--- a/solution.py
+++ b/solution.py
@@ -322,8 +322,8 @@
     last = send_direct(0)
     give_part(1)
     far_b = send_far(1)
+    last += send_passed(0, far_a)
     last += send_direct(1)
-    last += send_passed(0, far_a)
     last += send_passed(1, far_b)
     for p in range(2):
         for half in range(2):

time: 43.5 us -> 43.6 us (level)
    pallas_call x1, Pallas kernels: 39.2 us -> 38.7 us  [body(): pl.pallas_call(solve_kernel, out_shape=jax.ShapeDtypeStruct((ROWS // 4, C...]
    pallas_call x1, Pallas kernels: 2.71 us -> 3.19 us  [body(): pl.pallas_call(build_kernel, out_shape=jax.ShapeDtypeStruct((ROWS, WIDTH)...]
where the time goes in v8:
time: 43.6 us; the launch traced here: 43.4 us
  Pallas kernels  41.9 us (96%)
  between operations  0.77 us (2%)
  local copies, waits for them, and re-layouts  0.71 us (2%)
    pallas_call x1, Pallas kernels, body(): pl.pallas_call(solve_kernel, out_shape=jax.ShapeDtypeStruct((ROWS // 4, C...  38.7 us
    pallas_call x1, Pallas kernels, body(): pl.pallas_call(build_kernel, out_shape=jax.ShapeDtypeStruct((ROWS, WIDTH)...  3.19 us

profile of v8, /device:TPU:1, one launch (start us, length us, event | category | flops | bytes accessed | tf_op | source)
XLA Modules:
  0.0 43.4 jit_solution(15450309816688758698)
XLA Ops:
  0.0 0.0 copy-start
  0.7 3.2 %build_dense.1.dense = bf16[2048,1792]{1,0:T(8,128)(2,1)S(1)} custom-call(s32[1,1,96]{2,1,0:T(1,128)} %row_hbm.1, s32[1,1,96]{2,1,0:T(1,128)} %col_hbm.1, s32[1,1]{1,0:T(1,128)S(6)} %copy.7.count_ref, bf16[1,1,96,128,128]{4,3,2,1,0:T(8,128)(2,1)} %blocks_hbm.1), custom_call_target="tpu_custom_call" | custom-call | tf_op jit(solution)/shard_map/build_dense/pallas_call | solution.py:349
  3.9 0.0 copy-done
  4.0 38.7 %solve.1 = bf16[512,256]{1,0:T(8,128)(2,1)S(1)} custom-call(bf16[2048,1792]{1,0:T(8,128)(2,1)S(1)} %build_dense.1.dense, bf16[2048,256]{1,0:T(8,128)(2,1)S(1)} %copy-done), custom_call_target="tpu_custom_call" | custom-call | tf_op jit(solution)/shard_map/solve/pallas_call | solution.py:368
  42.7 0.7 %copy.8 = bf16[512,256]{1,0:T(8,128)(2,1)} copy(bf16[512,256]{1,0:T(8,128)(2,1)S(1)} %solve.1) | data formatting | bytes 524288
Async XLA Ops:
  0.0 3.9 %copy-start = (bf16[2048,256]{1,0:T(8,128)(2,1)S(1)}, bf16[2048,256]{1,0:T(8,128)(2,1)}, u32[]{:S(2)}) copy-start(bf16[2048,256]{1,0:T(8,128)(2,1)} %right.1) | copy-start | bytes 3145732
